TPU v7x, 256 devices: a whole 4x4x8 slice. The times are simulated.
256 devices in a mesh: tm: 32 (over x, y, z_hi), span: 8 (over z_lo, core).
Axes of the slice: x: 4, y: 4, z: 8 (z_hi: 2, z_lo: 4; z = z_hi * 4 + z_lo), core: 2. Of those that a mesh axis runs over, the one named last changes fastest.
Arguments:
- frames: bfloat16 [32, 64, 256, 128], P('tm', None, 'span'), may hold values from -6 to 6
- cotangent: bfloat16 [32, 64, 256, 128], P('tm', None, 'span'), may hold values from -6 to 6
- spatial_weight: bfloat16 [3, 3, 64, 64], replicated, may hold values from -0.25 to 0.25
- temporal_kernel: bfloat16 [64, 32], replicated, may hold values from -1 to 1
Outputs:
- block_output: bfloat16 [32, 64, 256, 128], P('tm', None, 'span')
- input_grad: bfloat16 [32, 64, 256, 128], P('tm', None, 'span')
- weight_grad: float32 [3, 3, 64, 64], replicated
- kernel_grad: float32 [64, 32], replicated
All inputs are finite; a program needn't handle non-finite values.
Results may differ from a plain program's by a relative error of at most 0.0051.
Values may be sent and summed in bfloat16 or wider, within the bound.
A program may use at most 64 MiB of HBM per device.

v0:
```python
import jax
import jax.numpy as jnp
from jax import lax
from jax.sharding import PartitionSpec as P


def padded_2(x, sides, width):
    for axis, dim in sides:
        size, length = (lax.axis_size(axis), x.shape[dim])
        up = [(i, (i + 1) % size) for i in range(size - 1)]
        down = [(j, i) for i, j in up]
        last = lax.slice_in_dim(x, length - width, length, axis=dim)
        first = lax.slice_in_dim(x, 0, width, axis=dim)
        before = lax.ppermute(last, axis, up)
        after = lax.ppermute(first, axis, down)
        x = jnp.concatenate([before, x, after], axis=dim)
    return x


def toeplitz(kernel):
    count = kernel.shape[1]
    chans = kernel.shape[0]
    vector = jnp.concatenate(
        [
            jnp.zeros((chans, 1), kernel.dtype),
            kernel[:, ::-1],
            jnp.zeros((chans, count - 1), kernel.dtype),
        ],
        axis=1,
    )
    tiled = jnp.tile(vector, (1, count))
    skewed = tiled[:, count : count + count * (2 * count - 1)].reshape(chans, count, 2 * count - 1)
    return skewed[:, :, :count]


def diagonal_sums(products):
    chans = products.shape[0]
    count = products.shape[1]
    flipped = products[:, :, ::-1]
    wide = jnp.concatenate([flipped, jnp.zeros_like(flipped)], axis=2)
    skewed = wide.reshape(chans, 2 * count * count)[:, : count * (2 * count - 1)].reshape(
        chans, count, 2 * count - 1
    )
    return jnp.sum(skewed[:, :, count - 1 :], axis=1)


def pad_chord(field):
    return jnp.pad(field, ((0, 0), (0, 0), (0, 0), (1, 1)))


def local(frames, cotangent, spatial_weight, temporal_kernel):
    local_steps, channels, rows, width = frames.shape
    frame_count = local_steps * lax.axis_size("tm")
    gscale = float(frame_count * rows * lax.axis_size("span") * width) ** (-0.5)
    padded = pad_chord(padded_2(frames, (("span", 2),), 1))
    hidden = jnp.zeros((local_steps, channels, rows, width), jnp.float32)
    for row_off in range(3):
        for col_off in range(3):
            slab = padded[:, :, row_off : row_off + rows, col_off : col_off + width]
            hidden = hidden + jnp.einsum(
                "oi,tisw->tosw",
                spatial_weight[row_off, col_off],
                slab,
                preferred_element_type=jnp.float32,
            )
    sigma = jax.nn.sigmoid(hidden)
    active = (hidden * sigma).astype(jnp.bfloat16)
    flat_act = active.reshape(local_steps, channels, rows * width)
    flat_cot = cotangent.reshape(local_steps, channels, rows * width)
    toe = toeplitz(temporal_kernel)
    tile_act = lax.all_to_all(flat_act, "tm", split_axis=2, concat_axis=0, tiled=True)
    back_along = lax.all_to_all(
        jnp.einsum("cts,scn->tcn", toe, tile_act, preferred_element_type=jnp.float32).astype(
            jnp.bfloat16
        ),
        "tm",
        split_axis=0,
        concat_axis=2,
        tiled=True,
    )
    tile_cot = lax.all_to_all(flat_cot, "tm", split_axis=2, concat_axis=0, tiled=True)
    back_grad = lax.all_to_all(
        jnp.einsum("cts,tcn->scn", toe, tile_cot, preferred_element_type=jnp.float32).astype(
            jnp.bfloat16
        ),
        "tm",
        split_axis=0,
        concat_axis=2,
        tiled=True,
    )
    lag_terms = diagonal_sums(
        jnp.einsum("tcn,scn->cts", tile_cot, tile_act, preferred_element_type=jnp.float32)
    )
    block_output = (
        frames.astype(jnp.float32) + back_along.reshape(frames.shape).astype(jnp.float32)
    ).astype(jnp.bfloat16)
    dhidden = (
        back_grad.reshape(frames.shape).astype(jnp.float32) * sigma * (1.0 + hidden * (1.0 - sigma))
    ).astype(jnp.bfloat16)
    dpadded = pad_chord(padded_2(dhidden, (("span", 2),), 1))
    grad_sum = cotangent.astype(jnp.float32)
    weight_terms = []
    for row_off in range(3):
        for col_off in range(3):
            dslab = dpadded[
                :, :, 2 - row_off : 2 - row_off + rows, 2 - col_off : 2 - col_off + width
            ]
            grad_sum = grad_sum + jnp.einsum(
                "oi,tosw->tisw",
                spatial_weight[row_off, col_off],
                dslab,
                preferred_element_type=jnp.float32,
            )
            slab = padded[:, :, row_off : row_off + rows, col_off : col_off + width]
            weight_terms.append(
                jnp.einsum("tosw,tisw->oi", dhidden, slab, preferred_element_type=jnp.float32)
            )
    input_grad = grad_sum.astype(jnp.bfloat16)
    weight_local = jnp.stack(weight_terms).reshape(3, 3, channels, channels)
    weight_total, kernel_total = lax.psum((weight_local, lag_terms), ("tm", "span"))
    return (block_output, input_grad, weight_total * gscale, kernel_total * gscale)


def solution(mesh):
    placed = (P("tm", None, "span", None), P("tm", None, "span", None), P(), P())
    return jax.shard_map(
        local,
        mesh=mesh,
        in_specs=placed,
        out_specs=(P("tm", None, "span", None), P("tm", None, "span", None), P(), P()),
        check_vma=False,
    )
```

profile of v0, /device:TPU:1, one launch (start us, length us, event | category | flops | bytes accessed | tf_op | source)
XLA Modules:
  0.0 456.6 jit_solution(3548482435631862121)
XLA Ops:
  7.2 1.3 copy.83
  8.5 4.9 %collective-permute-start = (bf16[1,64,1,128]{3,1,2,0:T(8,128)(2,1)S(1)}, bf16[1,64,1,128]{3,1,2,0:T(8,128)(2,1)S(1)}, u32[]{:S(2)}, u32[]{:S(2)}) collective-permute-start(bf16[1,64,1,128]{3,1,2,0:T(8,128)(2,1)S(1)} %get-tuple-element.24), channel_id=1, source_target_pairs={{0,1},{1,2},{2,3},{3,4},{4,5},{5,6},{6,7},{8,9},{9,10},{10,11},{11... | collective-permute-start | bytes 49160 | tf_op jit(solution)/shard_map/ppermute | solution.py:14
  13.5 1.9 collective-permute-start.1
  15.6 2.8 copy.96
  18.9 23.4 %reduce = bf16[4096,64]{1,0:T(8,128)(2,1)} reduce(bf16[4096,1,64]{2,1,0:T(2,128)(2,1)S(1)} %bitcast.335, bf16[]{:T(256)} %broadcast.43), dimensions={1}, to_apply=%bitcast.317.reduce_sub_computation | reduce | bytes 1048578
  42.3 3.0 reshape.197
  45.3 13.1 %all-to-all-start.2 = ((bf16[32,2,4096]{2,1,0:T(2,128)(2,1)}), bf16[32,2,4096]{2,1,0:T(2,128)(2,1)}, u32[]{:S(2)}, u32[]{:S(2)}) async-start(bf16[32,2,4096]{2,1,0:T(2,128)(2,1)} %reshape.197), calls=%async_computation.2 | async-start | bytes 1048576 | tf_op jit(solution)/shard_map/all_to_all | solution.py:81
  59.4 2.5 reshape.145
  63.4 1.3 convolution_add_fusion.4
  64.7 9.7 %all-to-all-done.2 = bf16[32,2,4096]{2,1,0:T(2,128)(2,1)} async-done(((bf16[32,2,4096]{2,1,0:T(2,128)(2,1)}), bf16[32,2,4096]{2,1,0:T(2,128)(2,1)}, u32[]{:S(2)}, u32[]{:S(2)}) %all-to-all-start.2) | async-done | bytes 524320 | tf_op jit(solution)/shard_map/all_to_all | solution.py:81
  74.4 4.1 reshape.198
  78.5 3.6 copy.97
  82.1 1.2 copy.137
  83.7 1.0 copy.147
  84.7 5.2 %all-to-all-start.3 = ((bf16[32,64,128]{2,1,0:T(8,128)(2,1)}), bf16[32,64,128]{2,1,0:T(8,128)(2,1)}, u32[]{:S(2)}, u32[]{:S(2)}) async-start(bf16[32,64,128]{2,1,0:T(8,128)(2,1)} %bitcast.346), calls=%async_computation.3 | async-start | bytes 1048576 | tf_op jit(solution)/shard_map/all_to_all | solution.py:82
  89.9 1.3 fusion.50
  92.0 1.3 convolution_add_fusion.1
  93.3 13.3 %all-to-all-done.3 = bf16[32,64,128]{2,1,0:T(8,128)(2,1)} async-done(((bf16[32,64,128]{2,1,0:T(8,128)(2,1)}), bf16[32,64,128]{2,1,0:T(8,128)(2,1)}, u32[]{:S(2)}, u32[]{:S(2)}) %all-to-all-start.3) | async-done | bytes 524320 | tf_op jit(solution)/shard_map/all_to_all | solution.py:82
  106.5 3.2 fusion.26
  112.6 8.1 %collective-permute-start.2 = (bf16[1,64,1,128]{3,1,2,0:T(8,128)(2,1)S(1)}, bf16[1,64,1,128]{3,1,2,0:T(8,128)(2,1)S(1)}, u32[]{:S(2)}, u32[]{:S(2)}) collective-permute-start(bf16[1,64,1,128]{3,1,2,0:T(8,128)(2,1)S(1)} %get-tuple-element.22), channel_id=1, source_target_pairs={{0,1},{1,2},{2,3},{3,4},{4,5},{5,6},{6,7},{8,9},{9,10},{10,11},{11... | collective-permute-start | bytes 49160 | tf_op jit(solution)/shard_map/ppermute | solution.py:14
  120.8 2.1 collective-permute-start.3
  123.3 1.3 copy.124
  124.6 6.9 %reshape.193 = bf16[1,64,4096]{1,0,2:T(2,128)(2,1)} reshape(bf16[1,64,32,128]{1,3,2,0:T(8,128)(2,1)} %copy.124) | data formatting | bytes 1048576 | tf_op jit(solution)/shard_map/reshape | solution.py:68
  131.5 24.4 %reduce.1 = bf16[4096,64]{1,0:T(8,128)(2,1)} reduce(bf16[4096,1,64]{2,1,0:T(2,128)(2,1)} %bitcast.336, bf16[]{:T(256)} %broadcast.43), dimensions={1}, to_apply=%bitcast.315.reduce_sub_computation | reduce | bytes 1048578
  156.0 3.0 reshape.195
  159.0 3.9 all-to-all-start
  163.5 1.4 convolution_bitcast_fusion.1
  164.8 1.3 convolution_bitcast_fusion
  166.1 1.4 convolution_bitcast_fusion.2
  167.5 1.4 convolution_bitcast_fusion.3
  168.9 1.4 convolution_bitcast_fusion.5
  170.3 1.4 convolution_bitcast_fusion.6
  171.6 1.5 fusion.3
  173.1 3.7 all-to-all-done
  176.8 3.6 reshape.196
  180.4 5.2 %copy.92 = bf16[1,64,4096]{2,1,0:T(8,128)(2,1)} copy(bf16[1,64,4096]{1,0,2:T(2,128)(2,1)} %bitcast.334) | data formatting | bytes 1048576 | tf_op jit(solution)/shard_map/all_to_all | solution.py:71
  185.6 1.1 copy.136
  187.0 1.0 copy.94
  188.0 8.0 %all-to-all-start.1 = ((bf16[32,64,128]{2,1,0:T(8,128)(2,1)}), bf16[32,64,128]{2,1,0:T(8,128)(2,1)S(1)}, u32[]{:S(2)}, u32[]{:S(2)}) async-start(bf16[32,64,128]{2,1,0:T(8,128)(2,1)} %copy.94), calls=%async_computation.1 | async-start | bytes 1048576 | tf_op jit(solution)/shard_map/all_to_all | solution.py:72
  196.0 3.8 fusion.12
  199.9 1.1 copy.112
  201.0 164.0 %all-reduce.5.cloned.1.call-done = f32[3,3,64,64]{3,2,1,0:T(8,128)} async-done(((f32[3,3,64,64]{3,2,1,0:T(8,128)}), f32[3,3,64,64]{3,2,1,0:T(8,128)}) %all-reduce.5.cloned.1.call-update) | async-done | bytes 147472 | tf_op jit(solution)/shard_map/psum | solution.py:120
  365.0 1.7 broadcast_multiply_fusion
  367.1 1.1 rev.7
  368.2 1.6 copy.135
  370.2 1.6 reshape.158
  372.1 75.6 %psum.15 = f32[64,32]{1,0:T(8,128)S(1)} all-reduce(f32[64,32]{1,0:T(8,128)S(1)} %slice_reduce_fusion), channel_id=1, replica_groups=mesh['tm'=32,'span'=8] {'tm','span'}, use_global_device_ids=true, to_apply=%region_2.3 | all-reduce | flops 2048 | bytes 16384 | tf_op jit(solution)/shard_map/psum | solution.py:120
  448.6 1.1 copy.111
  (72 shorter events, 10.5 us)
Async XLA Ops:
  7.2 8.2 %copy-start.7 = (bf16[1,64,32,128]{3,2,1,0:T(8,128)(2,1)S(1)}, bf16[1,64,32,128]{3,2,1,0:T(8,128)(2,1)}, u32[]{:S(2)}) copy-start(bf16[1,64,32,128]{3,2,1,0:T(8,128)(2,1)} %param.5) | copy-start | bytes 1572868
  8.5 54.3 %copy-start = (bf16[1,64,32,128]{3,1,2,0:T(8,128)(2,1)}, bf16[1,64,32,128]{3,1,2,0:T(8,128)(2,1)S(1)}, u32[]{:S(2)}) copy-start(bf16[1,64,32,128]{3,1,2,0:T(8,128)(2,1)S(1)} %copy.83) | copy-start | bytes 1572868
  8.5 53.4 %collective-permute-start = (bf16[1,64,1,128]{3,1,2,0:T(8,128)(2,1)S(1)}, bf16[1,64,1,128]{3,1,2,0:T(8,128)(2,1)S(1)}, u32[]{:S(2)}, u32[]{:S(2)}) collective-permute-start(bf16[1,64,1,128]{3,1,2,0:T(8,128)(2,1)S(1)} %get-tuple-element.24), channel_id=1, source_target_pairs={{0,1},{1,2},{2,3},{3,4},{4,5},{5,6},{6,7},{8,9},{9,10},{10,11},{11... | collective-permute-start | bytes 49160 | tf_op jit(solution)/shard_map/ppermute | solution.py:14
  13.5 48.4 %collective-permute-start.1 = (bf16[1,64,1,128]{3,1,2,0:T(8,128)(2,1)S(1)}, bf16[1,64,1,128]{3,1,2,0:T(8,128)(2,1)S(1)}, u32[]{:S(2)}, u32[]{:S(2)}) collective-permute-start(bf16[1,64,1,128]{3,1,2,0:T(8,128)(2,1)S(1)} %get-tuple-element.25), channel_id=1, source_target_pairs={{1,0},{2,1},{3,2},{4,3},{5,4},{6,5},{7,6},{9,8},{10,9},{11,10},{12... | collective-permute-start | bytes 49160 | tf_op jit(solution)/shard_map/ppermute | solution.py:15
  42.3 16.1 %copy-start.12 = (bf16[64,32]{0,1:T(8,128)(2,1)S(1)}, bf16[64,32]{0,1:T(8,128)(2,1)}, u32[]{:S(2)}) copy-start(bf16[64,32]{0,1:T(8,128)(2,1)} %param.7) | copy-start | bytes 12292
  45.3 29.0 %all-to-all-start.2 = ((bf16[32,2,4096]{2,1,0:T(2,128)(2,1)}), bf16[32,2,4096]{2,1,0:T(2,128)(2,1)}, u32[]{:S(2)}, u32[]{:S(2)}) async-start(bf16[32,2,4096]{2,1,0:T(2,128)(2,1)} %reshape.197), calls=%async_computation.2 | async-start | bytes 1048576 | tf_op jit(solution)/shard_map/all_to_all | solution.py:81
  59.4 3.0 copy-start.9
  82.1 1.2 copy-start.3
  83.3 1.4 copy-start.4
  84.7 6.6 %copy-start.2 = (bf16[1,64,32,128]{3,2,1,0:T(8,128)(2,1)S(1)}, bf16[1,64,32,128]{3,2,1,0:T(8,128)(2,1)}, u32[]{:S(2)}) copy-start(bf16[1,64,32,128]{3,2,1,0:T(8,128)(2,1)} %param.4) | copy-start | bytes 1572868
  84.7 6.6 %copy-start.6 = (f32[32,128,64]{1,2,0:T(8,128)S(1)}, f32[32,128,64]{1,2,0:T(8,128)}, u32[]{:S(2)}) copy-start(f32[32,128,64]{1,2,0:T(8,128)} %convolution_add_fusion.4) | copy-start | bytes 3145732
  84.7 21.9 %all-to-all-start.3 = ((bf16[32,64,128]{2,1,0:T(8,128)(2,1)}), bf16[32,64,128]{2,1,0:T(8,128)(2,1)}, u32[]{:S(2)}, u32[]{:S(2)}) async-start(bf16[32,64,128]{2,1,0:T(8,128)(2,1)} %bitcast.346), calls=%async_computation.3 | async-start | bytes 1048576 | tf_op jit(solution)/shard_map/all_to_all | solution.py:82
  89.9 275.1 %all-reduce.5.cloned.1.call-start = ((), (), s32[]{:S(2)}) async-start(), calls=%async_computation.4 | async-start | bytes 589824 | tf_op jit(solution)/shard_map/psum | solution.py:120
  92.0 14.6 %copy-start.1 = (bf16[1,64,32,128]{3,1,2,0:T(8,128)(2,1)S(1)}, bf16[1,64,32,128]{3,1,2,0:T(8,128)(2,1)}, u32[]{:S(2)}) copy-start(bf16[1,64,32,128]{3,1,2,0:T(8,128)(2,1)} %copy-done) | copy-start | bytes 1572868
  112.6 8.2 %copy-start.11 = (f32[9,64,64]{2,1,0:T(8,128)}, f32[9,64,64]{2,1,0:T(8,128)S(1)}, u32[]{:S(2)}) copy-start(f32[9,64,64]{2,1,0:T(8,128)S(1)} %fusion.15) | copy-start | bytes 442372
  112.6 10.7 %copy-start.10 = (bf16[1,64,32,128]{3,1,2,0:T(8,128)(2,1)S(1)}, bf16[1,64,32,128]{3,1,2,0:T(8,128)(2,1)}, u32[]{:S(2)}) copy-start(bf16[1,64,32,128]{3,1,2,0:T(8,128)(2,1)} %get-tuple-element.21) | copy-start | bytes 1572868
  112.6 50.2 %collective-permute-start.2 = (bf16[1,64,1,128]{3,1,2,0:T(8,128)(2,1)S(1)}, bf16[1,64,1,128]{3,1,2,0:T(8,128)(2,1)S(1)}, u32[]{:S(2)}, u32[]{:S(2)}) collective-permute-start(bf16[1,64,1,128]{3,1,2,0:T(8,128)(2,1)S(1)} %get-tuple-element.22), channel_id=1, source_target_pairs={{0,1},{1,2},{2,3},{3,4},{4,5},{5,6},{6,7},{8,9},{9,10},{10,11},{11... | collective-permute-start | bytes 49160 | tf_op jit(solution)/shard_map/ppermute | solution.py:14
  120.8 42.1 %collective-permute-start.3 = (bf16[1,64,1,128]{3,1,2,0:T(8,128)(2,1)S(1)}, bf16[1,64,1,128]{3,1,2,0:T(8,128)(2,1)S(1)}, u32[]{:S(2)}, u32[]{:S(2)}) collective-permute-start(bf16[1,64,1,128]{3,1,2,0:T(8,128)(2,1)S(1)} %get-tuple-element.23), channel_id=1, source_target_pairs={{1,0},{2,1},{3,2},{4,3},{5,4},{6,5},{7,6},{9,8},{10,9},{11,10},{12... | collective-permute-start | bytes 49160 | tf_op jit(solution)/shard_map/ppermute | solution.py:15
  159.0 17.8 %all-to-all-start = ((bf16[32,2,4096]{2,1,0:T(2,128)(2,1)}), bf16[32,2,4096]{2,1,0:T(2,128)(2,1)S(1)}, u32[]{:S(2)}, u32[]{:S(2)}) async-start(bf16[32,2,4096]{2,1,0:T(2,128)(2,1)} %reshape.195), calls=%async_computation | async-start | bytes 1048576 | tf_op jit(solution)/shard_map/all_to_all | solution.py:71
  170.3 1.4 copy-start.8
  188.0 260.4 %all-to-all-start.1 = ((bf16[32,64,128]{2,1,0:T(8,128)(2,1)}), bf16[32,64,128]{2,1,0:T(8,128)(2,1)S(1)}, u32[]{:S(2)}, u32[]{:S(2)}) async-start(bf16[32,64,128]{2,1,0:T(8,128)(2,1)} %copy.94), calls=%async_computation.1 | async-start | bytes 1048576 | tf_op jit(solution)/shard_map/all_to_all | solution.py:72
  199.8 166.8 %copy-start.5 = (bf16[8,8,32,128]{3,2,1,0:T(8,128)(2,1)S(1)}, bf16[8,8,32,128]{3,2,1,0:T(8,128)(2,1)}, u32[]{:S(2)}) copy-start(bf16[8,8,32,128]{3,2,1,0:T(8,128)(2,1)} %copy-done.4) | copy-start | bytes 1572868
Sparse Core Ops, SparseCore 0:
  123.4 241.5 all-reduce.4
where the time goes:
time: 458 us; the launch traced here: 457 us
  waiting for transfers between devices  191 us (42%)
  blocking collectives  75.6 us (17%)
  other arithmetic  51.3 us (11%)
  local copies, waits for them, and re-layouts  51 us (11%)
  starting transfers between devices  47.3 us (10%)
  matrix products  26.3 us (6%)
  between operations  14.5 us (3%)
    psum x1, waiting for transfers between devices, local(): lax.psum((weight_local, lag_terms), ('tm', 'span'))  164 us
    psum x1, blocking collectives, local(): lax.psum((weight_local, lag_terms), ('tm', 'span'))  75.6 us
    unnamed x2, other arithmetic  47.8 us
    unnamed x38, local copies, waits for them, and re-layouts  22.5 us
    dot_general x9, matrix products, local(): jnp.einsum('oi,tosw->tisw', spatial_weight[row_off, col_off], dslab, pref...  13.8 us
    all_to_all x1, waiting for transfers between devices, local(): lax.all_to_all(jnp.einsum('cts,tcn->scn', toe, tile_cot, preferred_elemen...  13.3 us
    all_to_all x1, starting transfers between devices, local(): lax.all_to_all(flat_cot, 'tm', split_axis=2, concat_axis=0, tiled=True)  13.1 us
    ppermute x2, starting transfers between devices, padded_2(): before = lax.ppermute(last, axis, up)  13.1 us
  transfers between devices with their start and end apart: 9, of which 4 were waited for; matrix products, arithmetic and copies ran while one was open for 24% of the time, Pallas kernels for 0%

commit v1 on v0

v1 whole, which is shorter than its diff:
```python
import functools

import jax
import jax.numpy as jnp
from jax import lax
from jax.experimental import pallas as pl
from jax.experimental.pallas import tpu as pltpu
from jax.sharding import PartitionSpec as P

F32 = jnp.float32
BF16 = jnp.bfloat16
MESH = pl.DeviceIdType.MESH
LANES = 128
BLK = 8


def causal_sums(n, x_at, k_at, put):
    for tb in range(0, n, BLK):
        acc = [None] * BLK
        for rb in range(0, tb + BLK, BLK):
            xs = [x_at(rb + j) for j in range(BLK)]
            ks = {}
            for lag in range(max(0, tb - rb - BLK + 1), tb - rb + BLK):
                ks[lag] = k_at(lag)
            for i in range(BLK):
                for j in range(BLK):
                    lag = tb + i - rb - j
                    if lag >= 0:
                        term = ks[lag] * xs[j]
                        acc[i] = term if acc[i] is None else acc[i] + term
        for i in range(BLK):
            put(tb + i, acc[i])


def lag_sums(n, t_at, r_at, put):
    acc = {}
    for dist in range(0, n, BLK):
        for rb in range(0, n - dist, BLK):
            ts = [t_at(rb + dist + i) for i in range(BLK)]
            rs = [r_at(rb + j) for j in range(BLK)]
            for i in range(BLK):
                for j in range(BLK):
                    lag = dist + i - j
                    if lag >= 0:
                        term = ts[i] * rs[j]
                        acc[lag] = acc[lag] + term if lag in acc else term
        for lag in sorted(acc):
            if lag <= dist:
                put(lag, acc.pop(lag))
    for lag in sorted(acc):
        put(lag, acc.pop(lag))


def kernel(
    n,
    nspan,
    gscale,
    frames_ref,
    cot_ref,
    wf_ref,
    wb_ref,
    temporal_ref,
    block_ref,
    input_grad_ref,
    weight_grad_ref,
    kernel_grad_ref,
    tmp,
    xp,
    x3,
    cot_t,
    act_t,
    gbuf,
    kb,
    rcot,
    ract,
    xf,
    yf,
    outf,
    back_t,
    along_t,
    rback,
    ralong,
    dp,
    db,
    igf,
    kgbuf,
    red,
    rred,
    part,
    zpart,
    full,
    gathered,
    send_sems,
    recv_sems,
):
    me = lax.axis_index("tm")
    sp = lax.axis_index("span")
    xy, zh = me // 2, me % 2
    zl, core = sp // 2, sp % 2
    zcount = nspan
    zi = zh * (nspan // 2) + zl
    pi = xy * 2 + core
    ch = 64

    def tm_dev(t):
        return (t, sp)

    def plane_dev(p):
        return ((p // 2) * 2 + zh, zl * 2 + p % 2)

    def z_dev(z):
        return (xy * 2 + z // (nspan // 2), (z % (nspan // 2)) * 2 + core)

    barrier = pltpu.get_barrier_semaphore()

    def greet(dev):
        pl.semaphore_signal(barrier, inc=1, device_id=dev, device_id_type=MESH)

    @pl.loop(1, n)
    def _(k):
        greet(tm_dev(lax.rem(me + k, n)))

    @pl.loop(0, n // 2)
    def _(k):
        greet(plane_dev(2 * lax.rem(xy + k, n // 2) + 1 - core))

    @pl.loop(1, zcount // 2)
    def _(k):
        greet(z_dev(lax.rem(zi + k, zcount)))
        greet(z_dev(lax.rem(zi + zcount - k, zcount)))

    greet((me, lax.rem(sp + 1, nspan)))
    greet((me, lax.rem(sp + nspan - 1, nspan)))

    lane = lax.broadcasted_iota(jnp.int32, (ch, LANES), 1)

    def right(v):
        return jnp.where(lane == 0, 0.0, pltpu.roll(v, 1, 1))

    def left(v):
        return jnp.where(lane == LANES - 1, 0.0, pltpu.roll(v, LANES - 1, 1))

    @pl.loop(0, ch)
    def _(c):
        tmp[pl.ds(c, n, stride=ch), :] = cot_ref[0, c].astype(F32)

    @pl.loop(0, n)
    def _(r):
        cot_t[r] = tmp[pl.ds(pl.multiple_of(r * ch, ch), ch), :].astype(BF16)

    @pl.loop(0, ch)
    def _(c):
        tmp[pl.ds(c, n, stride=ch), :] = frames_ref[0, c].astype(F32)

    @pl.loop(0, n)
    def _(r):
        xp[r + 1] = tmp[pl.ds(pl.multiple_of(r * ch, ch), ch), :].astype(BF16)

    @pl.when(sp == 0)
    def _():
        xp[0] = jnp.zeros((ch, LANES), BF16)
        dp[0] = jnp.zeros((ch, LANES), BF16)

    @pl.when(sp == nspan - 1)
    def _():
        xp[n + 1] = jnp.zeros((ch, LANES), BF16)
        dp[n + 1] = jnp.zeros((ch, LANES), BF16)

    def row_cols(s):
        return pl.ds(pl.multiple_of(s * LANES, LANES), LANES)

    def load_taps(s):
        for a in range(3):
            x3[a * ch : (a + 1) * ch, row_cols(s)] = xp[s + a]

    def forward_rows(rows):
        taps = jnp.concatenate([x3[:, row_cols(s)] for s in rows], axis=1)
        out = jnp.dot(wf_ref[...], taps, preferred_element_type=F32)
        for k, s in enumerate(rows):
            o = out[:, k * LANES : (k + 1) * LANES]
            hidden = o[ch : 2 * ch] + right(o[:ch]) + left(o[2 * ch :])
            sigma = jax.nn.sigmoid(hidden)
            act_t[s] = (hidden * sigma).astype(BF16)
            gbuf[s] = sigma * (1.0 + hidden * (1.0 - sigma))

    @pl.loop(1, n - 1)
    def _(s):
        load_taps(s)

    @pl.loop(0, (n - 2) // 2)
    def _(p):
        forward_rows([1 + 2 * p, 2 + 2 * p])

    pl.semaphore_wait(barrier, n - 1 + n // 2 + 2 * (zcount // 2 - 1) + 2)

    def exchange(src, dst, idx, k):
        peer = lax.rem(me + k, n)
        return pltpu.make_async_remote_copy(
            src_ref=src.at[peer],
            dst_ref=dst.at[me],
            send_sem=send_sems.at[idx],
            recv_sem=recv_sems.at[idx],
            device_id=tm_dev(peer),
            device_id_type=MESH,
        )

    def start_exchange(src, dst, idx):
        @pl.loop(0, n // 2)
        def _(k):
            exchange(src, dst, idx, 2 * k + 1).start()

        @pl.loop(1, n // 2)
        def _(k):
            exchange(src, dst, idx, 2 * k).start()

        dst[me] = src[me]

    def all_of(buf, count, idx):
        view = buf.at[pl.ds(0, count)]
        return pltpu.make_async_remote_copy(
            src_ref=view,
            dst_ref=view,
            send_sem=send_sems.at[idx],
            recv_sem=recv_sems.at[idx],
            device_id=tm_dev(lax.rem(me + 1, n)),
            device_id_type=MESH,
        )

    def halo(buf, idx):
        up = pltpu.make_async_remote_copy(
            src_ref=buf.at[n],
            dst_ref=buf.at[0],
            send_sem=send_sems.at[idx],
            recv_sem=recv_sems.at[idx],
            device_id=(me, sp + 1),
            device_id_type=MESH,
        )
        down = pltpu.make_async_remote_copy(
            src_ref=buf.at[1],
            dst_ref=buf.at[n + 1],
            send_sem=send_sems.at[idx + 1],
            recv_sem=recv_sems.at[idx + 1],
            device_id=(me, sp - 1),
            device_id_type=MESH,
        )
        return up, down

    def start_halo(buf, idx):
        up, down = halo(buf, idx)

        @pl.when(sp < nspan - 1)
        def _():
            up.start()

        @pl.when(sp > 0)
        def _():
            down.start()

    def finish_halo(buf, idx):
        up, down = halo(buf, idx)

        @pl.when(sp > 0)
        def _():
            up.wait_recv()

        @pl.when(sp < nspan - 1)
        def _():
            down.wait_recv()

        @pl.when(sp < nspan - 1)
        def _():
            up.wait_send()

        @pl.when(sp > 0)
        def _():
            down.wait_send()

    start_halo(xp, 0)
    start_exchange(cot_t, rcot, 4)
    finish_halo(xp, 0)
    load_taps(0)
    load_taps(n - 1)
    forward_rows([0, n - 1])
    start_exchange(act_t, ract, 5)

    for lag in range(n):
        kb[lag] = jnp.broadcast_to(temporal_ref[:, lag : lag + 1].astype(F32), (ch, LANES))

    def chan(c):
        return pl.ds(pl.multiple_of(c * 8, 8), 8)

    all_of(rcot, n - 1, 4).wait_recv()

    @pl.loop(0, n)
    def _(t):
        yf[t] = rcot[t].astype(F32)

    @pl.loop(0, ch // 8)
    def _(c):
        def put(t, v):
            outf[n - 1 - t, chan(c), :] = v

        causal_sums(n, lambda t: yf[n - 1 - t, chan(c), :], lambda lag: kb[lag, chan(c), :], put)

    @pl.loop(0, n)
    def _(t):
        back_t[t] = outf[t].astype(BF16)

    start_exchange(back_t, rback, 6)

    all_of(ract, n - 1, 5).wait_recv()

    @pl.loop(0, n)
    def _(t):
        xf[t] = ract[t].astype(F32)

    @pl.loop(0, ch // 8)
    def _(c):
        def put(t, v):
            outf[t, chan(c), :] = v

        causal_sums(n, lambda t: xf[t, chan(c), :], lambda lag: kb[lag, chan(c), :], put)

    @pl.loop(0, n)
    def _(t):
        along_t[t] = outf[t].astype(BF16)

    start_exchange(along_t, ralong, 7)

    lane8 = lax.broadcasted_iota(jnp.int32, (8, 2 * LANES), 1)

    @pl.loop(0, ch // 8)
    def _(c):
        total = [jnp.zeros((8, 2 * LANES), F32)]

        def put(lag, v):
            row = jnp.sum(v, axis=1, keepdims=True)
            total[0] = jnp.where(lane8 == lag, row, total[0])

        lag_sums(n, lambda t: yf[t, chan(c), :], lambda r: xf[r, chan(c), :], put)
        kgbuf[chan(c), :] = total[0]

    all_of(rback, n - 1, 6).wait_recv()

    def gate_row(s):
        v = rback[s].astype(F32) * gbuf[s]
        dp[s + 1] = v.astype(BF16)
        db[:ch, row_cols(s)] = left(v).astype(BF16)
        db[ch : 2 * ch, row_cols(s)] = v.astype(BF16)
        db[2 * ch :, row_cols(s)] = right(v).astype(BF16)

    gate_row(0)
    gate_row(n - 1)
    start_halo(dp, 2)

    @pl.loop(1, n - 1)
    def _(s):
        gate_row(s)

    grads = lax.dot_general(
        db[...], x3[...], (((1,), (1,)), ((), ())), preferred_element_type=F32
    )
    per = 192 // n
    kper = ch // n
    grads = jnp.concatenate([grads, jnp.zeros((192, 64), F32)], axis=1)
    for k in range(n):
        red[k, 0:per, :] = grads[k * per : (k + 1) * per]
        red[k, per : per + kper, :] = kgbuf[k * kper : (k + 1) * kper, :]

    def plane_copy(src, dst, idx, peer):
        return pltpu.make_async_remote_copy(
            src_ref=src,
            dst_ref=dst.at[pi],
            send_sem=send_sems.at[idx],
            recv_sem=recv_sems.at[idx],
            device_id=plane_dev(peer),
            device_id_type=MESH,
        )

    @pl.loop(1, n)
    def _(k):
        peer = lax.rem(pi + k, n)
        plane_copy(red.at[peer], rred, 8, peer).start()

    rred[pi] = red[pi]

    def backward_rows(rows):
        taps = jnp.concatenate(
            [jnp.concatenate([dp[s + j] for j in range(3)], axis=0) for s in rows], axis=1
        )
        out = jnp.dot(wb_ref[...], taps, preferred_element_type=F32)
        for k, s in enumerate(rows):
            o = out[:, k * LANES : (k + 1) * LANES]
            igf[pl.ds(pl.multiple_of(s * ch, ch), ch), :] = (
                o[ch : 2 * ch] + left(o[:ch]) + right(o[2 * ch :])
            )

    @pl.loop(0, (n - 2) // 2)
    def _(p):
        backward_rows([1 + 2 * p, 2 + 2 * p])

    all_of(rred, n - 1, 8).wait_recv()
    part[...] = jnp.sum(rred[...], axis=0)

    def z_copy(k):
        peer = lax.rem(zi + k, zcount)
        return pltpu.make_async_remote_copy(
            src_ref=part,
            dst_ref=zpart.at[zi],
            send_sem=send_sems.at[9],
            recv_sem=recv_sems.at[9],
            device_id=z_dev(peer),
            device_id_type=MESH,
        )

    @pl.loop(1, zcount)
    def _(k):
        z_copy(k).start()

    zpart[zi] = part[...]

    finish_halo(dp, 2)
    backward_rows([0, n - 1])

    all_of(zpart, zcount - 1, 9).wait_recv()
    full[...] = jnp.sum(zpart[...], axis=0) * gscale

    @pl.loop(1, n)
    def _(k):
        peer = lax.rem(pi + k, n)
        plane_copy(full, gathered, 10, peer).start()

    gathered[pi] = full[...]

    @pl.loop(0, ch)
    def _(c):
        input_grad_ref[0, c] = (
            cot_ref[0, c].astype(F32) + igf[pl.ds(c, n, stride=ch), :]
        ).astype(BF16)

    all_of(ralong, n - 1, 7).wait_recv()

    @pl.loop(0, n)
    def _(r):
        tmp[pl.ds(pl.multiple_of(r * ch, ch), ch), :] = ralong[r].astype(F32)

    @pl.loop(0, ch)
    def _(c):
        block_ref[0, c] = (
            frames_ref[0, c].astype(F32) + tmp[pl.ds(c, n, stride=ch), :]
        ).astype(BF16)

    all_of(gathered, n - 1, 10).wait_recv()
    whole = jnp.concatenate([gathered[k, 0:per, :] for k in range(n)], axis=0)
    for a in range(3):
        for b in range(3):
            weight_grad_ref[a, b] = whole[b * ch : (b + 1) * ch, a * ch : (a + 1) * ch]
    kernel_grad_ref[...] = jnp.concatenate(
        [gathered[k, per : per + kper, 0:n] for k in range(n)], axis=0
    )

    all_of(rcot, n - 1, 4).wait_send()
    all_of(ract, n - 1, 5).wait_send()
    all_of(rback, n - 1, 6).wait_send()
    all_of(ralong, n - 1, 7).wait_send()
    all_of(rred, n - 1, 8).wait_send()
    all_of(zpart, zcount - 1, 9).wait_send()
    all_of(gathered, n - 1, 10).wait_send()


def local(frames, cotangent, spatial_weight, temporal_kernel):
    n = lax.axis_size("tm")
    nspan = lax.axis_size("span")
    _, ch, rows, width = frames.shape
    assert rows == n and ch == 64 and width == LANES and frames.shape[0] == 1
    gscale = float(n * rows * nspan * width) ** (-0.5)
    wf = spatial_weight.transpose(1, 2, 0, 3).reshape(3 * ch, 3 * ch)
    wb = spatial_weight[::-1].transpose(1, 3, 0, 2).reshape(3 * ch, 3 * ch)
    block = (n, ch, LANES)
    red = (n, 256 // n, 256)

    def vmem(shape, dtype):
        return pltpu.VMEM(shape, dtype)

    spec = pl.BlockSpec(memory_space=pltpu.VMEM)
    return pl.pallas_call(
        functools.partial(kernel, n, nspan, gscale),
        name="space_time_block",
        out_shape=(
            jax.ShapeDtypeStruct(frames.shape, BF16),
            jax.ShapeDtypeStruct(frames.shape, BF16),
            jax.ShapeDtypeStruct((3, 3, ch, ch), F32),
            jax.ShapeDtypeStruct((ch, n), F32),
        ),
        in_specs=[spec] * 5,
        out_specs=(spec,) * 4,
        scratch_shapes=[
            vmem((n * ch, LANES), F32),
            vmem((n + 2, ch, LANES), BF16),
            vmem((3 * ch, n * LANES), BF16),
            vmem(block, BF16),
            vmem(block, BF16),
            vmem(block, F32),
            vmem(block, F32),
            vmem(block, BF16),
            vmem(block, BF16),
            vmem(block, F32),
            vmem(block, F32),
            vmem(block, F32),
            vmem(block, BF16),
            vmem(block, BF16),
            vmem(block, BF16),
            vmem(block, BF16),
            vmem((n + 2, ch, LANES), BF16),
            vmem((3 * ch, n * LANES), BF16),
            vmem((n * ch, LANES), F32),
            vmem((ch, 256), F32),
            vmem(red, F32),
            vmem(red, F32),
            vmem(red[1:], F32),
            vmem((nspan,) + red[1:], F32),
            vmem(red[1:], F32),
            vmem(red, F32),
            pltpu.SemaphoreType.DMA((11,)),
            pltpu.SemaphoreType.DMA((11,)),
        ],
        compiler_params=pltpu.CompilerParams(
            collective_id=0, has_side_effects=True, vmem_limit_bytes=48 * 2**20
        ),
    )(frames, cotangent, wf, wb, temporal_kernel)


def solution(mesh):
    placed = (P("tm", None, "span", None), P("tm", None, "span", None), P(), P())
    return jax.shard_map(
        local,
        mesh=mesh,
        in_specs=placed,
        out_specs=placed,
        check_vma=False,
    )
```

time: 458 us -> 84.9 us (0.19)
  waiting for transfers between devices: 191 us -> 0 us
  Pallas kernels: 0 us -> 78.1 us
  blocking collectives: 75.6 us -> 0 us
  other arithmetic: 51.3 us -> 0 us
  starting transfers between devices: 47.3 us -> 0 us
  local copies, waits for them, and re-layouts: 51 us -> 5.99 us
  matrix products: 26.3 us -> 0 us
  between operations: 14.5 us -> 0.68 us
    psum x1 -> x0, waiting for transfers between devices: 164 us -> none  [local(): lax.psum((weight_local, lag_terms), ('tm', 'span'))]
    pallas_call x0 -> x1, Pallas kernels: none -> 78.1 us  [local(): pl.pallas_call(functools.partial(kernel, n, nspan, gscale), name='space_t...]
    psum x1 -> x0, blocking collectives: 75.6 us -> none  [local(): lax.psum((weight_local, lag_terms), ('tm', 'span'))]
    unnamed x2 -> x0, other arithmetic: 47.8 us -> none
    all_to_all x4 -> x0, starting transfers between devices: 30.1 us -> none  [the longest x1 13.1 us: local(): lax.all_to_all(flat_cot, 'tm', split_axis=2, concat_axis=0, tiled=True)]
    all_to_all x4 -> x0, waiting for transfers between devices: 26.6 us -> none  [the longest x1 13.3 us: local(): lax.all_to_all(jnp.einsum('cts,tcn->scn', toe, tile_cot, preferred_elemen...]
    dot_general x30 -> x0, matrix products: 26.3 us -> none  [the longest x9 13.8 us: local(): jnp.einsum('oi,tosw->tisw', spatial_weight[row_off, col_off], dslab, pref...]
    unnamed x38 -> x10, local copies, waits for them, and re-layouts: 22.5 us -> 3.7 us
  transfers between devices with their start and end apart: 9 -> 0, of which waited for: 4 -> 0; matrix products, arithmetic and copies ran while one was open for 24% -> 0% of each run, Pallas kernels for 0% -> 0%
where the time goes in v1:
time: 84.9 us; the launch traced here: 84.7 us
  Pallas kernels  78.1 us (92%)
  local copies, waits for them, and re-layouts  5.99 us (7%)
    pallas_call x1, Pallas kernels, local(): pl.pallas_call(functools.partial(kernel, n, nspan, gscale), name='space_t...  78.1 us
    unnamed x10, local copies, waits for them, and re-layouts  3.7 us

profile of v1, /device:TPU:1, one launch (start us, length us, event | category | flops | bytes accessed | tf_op | source)
XLA Modules:
  0.0 84.7 jit_solution(16636662378567694105)
XLA Ops:
  0.6 0.8 copy.14.temporal_ref
  1.4 0.0 copy-start.2
  1.4 1.0 %reverse_bitcast_fusion = bf16[3,64,3,64]{1,3,0,2:T(8,128)(2,1)S(1)} fusion(bf16[3,3,64,64]{3,2,1,0:T(8,128)(2,1)} %param.6), kind=kLoop, calls=%fused_computation | loop fusion | bytes 147456 | tf_op jit(solution)/shard_map/transpose | solution.py:478
  2.4 0.0 copy-start.1
  2.4 0.2 copy.13
  2.6 0.0 copy-start
  2.6 0.2 reshape.15.wb_ref
  2.8 0.0 copy-done.2
  2.8 0.1 copy.12
  2.9 0.2 reshape.14.wf_ref
  3.1 0.4 copy-done.1
  3.5 0.2 copy-done
  3.7 78.1 %space_time_block.1 = (bf16[1,64,32,128]{3,2,1,0:T(8,128)(2,1)S(1)}, bf16[1,64,32,128]{3,2,1,0:T(8,128)(2,1)S(1)}, f32[3,3,64,64]{3,2,1,0:T(8,128)S(1)}, f32[64,32]{1,0:T(8,128)S(1)}) custom-call(bf16[1,64,32,128]{3,2,1,0:T(8,128)(2,1)S(1)} %copy-done, bf16[1,64,32,128]{3,2,1,0:T(8,128)(2,1)S(1)} %copy-done.1, bf16[192,192]{1,0:T(8,128)(2,1)S(1)} %reshape.14.wf_ref, ...), custom_call_target="tpu_custom_call" | custom-call | tf_op jit(solution)/shard_map/space_time_block/pallas_call | solution.py:486
  81.8 0.7 copy.15
  82.4 0.8 copy.19
  83.2 0.8 copy.20
  84.0 0.7 copy.21
Async XLA Ops:
  1.4 1.4 %copy-start.2 = (bf16[3,3,64,64]{3,2,1,0:T(8,128)(2,1)S(1)}, bf16[3,3,64,64]{3,2,1,0:T(8,128)(2,1)}, u32[]{:S(2)}) copy-start(bf16[3,3,64,64]{3,2,1,0:T(8,128)(2,1)} %param.6) | copy-start | bytes 221188
  2.4 1.0 %copy-start.1 = (bf16[1,64,32,128]{3,2,1,0:T(8,128)(2,1)S(1)}, bf16[1,64,32,128]{3,2,1,0:T(8,128)(2,1)}, u32[]{:S(2)}) copy-start(bf16[1,64,32,128]{3,2,1,0:T(8,128)(2,1)} %cot_ref.1) | copy-start | bytes 1572868
  2.6 1.1 %copy-start = (bf16[1,64,32,128]{3,2,1,0:T(8,128)(2,1)S(1)}, bf16[1,64,32,128]{3,2,1,0:T(8,128)(2,1)}, u32[]{:S(2)}) copy-start(bf16[1,64,32,128]{3,2,1,0:T(8,128)(2,1)} %frames_ref.1) | copy-start | bytes 1572868

commit v2 on v1

--- a/solution.py
+++ b/solution.py
@@ -55,16 +55,21 @@
     n,
     nspan,
     gscale,
-    frames_ref,
-    cot_ref,
-    wf_ref,
-    wb_ref,
-    temporal_ref,
+    frames_hbm,
+    cot_hbm,
+    weight_hbm,
+    temporal_hbm,
     block_ref,
     input_grad_ref,
     weight_grad_ref,
     kernel_grad_ref,
+    frames_ref,
+    cot_ref,
+    weight_ref,
+    temporal_ref,
     tmp,
+    wf,
+    wb,
     xp,
     x3,
     cot_t,
@@ -84,6 +89,8 @@
     db,
     igf,
     kgbuf,
+    kz,
+    kp,
     red,
     rred,
     part,
@@ -92,6 +99,7 @@
     gathered,
     send_sems,
     recv_sems,
+    load_sems,
 ):
     me = lax.axis_index("tm")
     sp = lax.axis_index("span")
@@ -111,6 +119,20 @@
     def z_dev(z):
         return (xy * 2 + z // (nspan // 2), (z % (nspan // 2)) * 2 + core)
 
+    loads = [
+        pltpu.make_async_copy(src, dst, load_sems.at[k])
+        for k, (src, dst) in enumerate(
+            [
+                (cot_hbm, cot_ref),
+                (frames_hbm, frames_ref),
+                (weight_hbm, weight_ref),
+                (temporal_hbm, temporal_ref),
+            ]
+        )
+    ]
+    for load in loads:
+        load.start()
+
     barrier = pltpu.get_barrier_semaphore()
 
     def greet(dev):
@@ -140,21 +162,30 @@
     def left(v):
         return jnp.where(lane == LANES - 1, 0.0, pltpu.roll(v, LANES - 1, 1))
 
-    @pl.loop(0, ch)
-    def _(c):
-        tmp[pl.ds(c, n, stride=ch), :] = cot_ref[0, c].astype(F32)
-
-    @pl.loop(0, n)
-    def _(r):
-        cot_t[r] = tmp[pl.ds(pl.multiple_of(r * ch, ch), ch), :].astype(BF16)
-
-    @pl.loop(0, ch)
-    def _(c):
-        tmp[pl.ds(c, n, stride=ch), :] = frames_ref[0, c].astype(F32)
-
-    @pl.loop(0, n)
-    def _(r):
-        xp[r + 1] = tmp[pl.ds(pl.multiple_of(r * ch, ch), ch), :].astype(BF16)
+    def rows_first(src, dst, offset):
+        @pl.loop(0, ch, unroll=8)
+        def _(c):
+            tmp[pl.ds(c, n, stride=ch), :] = src[0, c].astype(F32)
+
+        @pl.loop(0, n, unroll=4)
+        def _(r):
+            dst[r + offset] = tmp[pl.ds(pl.multiple_of(r * ch, ch), ch), :].astype(BF16)
+
+    loads[0].wait()
+    rows_first(cot_ref, cot_t, 0)
+    loads[1].wait()
+    rows_first(frames_ref, xp, 1)
+    loads[2].wait()
+    loads[3].wait()
+
+    wide = []
+    for b in range(3):
+        wide.append(jnp.concatenate([weight_ref[a, b].astype(F32) for a in range(3)], axis=1))
+    wf[...] = jnp.concatenate(wide, axis=0).astype(BF16)
+    wide = []
+    for j in range(3):
+        wide.append(jnp.concatenate([weight_ref[2 - j, b].astype(F32) for b in range(3)], axis=1))
+    wb[...] = jnp.concatenate(wide, axis=0).T.astype(BF16)
 
     @pl.when(sp == 0)
     def _():
@@ -175,7 +206,7 @@
 
     def forward_rows(rows):
         taps = jnp.concatenate([x3[:, row_cols(s)] for s in rows], axis=1)
-        out = jnp.dot(wf_ref[...], taps, preferred_element_type=F32)
+        out = jnp.dot(wf[...], taps, preferred_element_type=F32)
         for k, s in enumerate(rows):
             o = out[:, k * LANES : (k + 1) * LANES]
             hidden = o[ch : 2 * ch] + right(o[:ch]) + left(o[2 * ch :])
@@ -183,40 +214,36 @@
             act_t[s] = (hidden * sigma).astype(BF16)
             gbuf[s] = sigma * (1.0 + hidden * (1.0 - sigma))
 
-    @pl.loop(1, n - 1)
+    @pl.loop(1, n - 1, unroll=2)
     def _(s):
         load_taps(s)
 
-    @pl.loop(0, (n - 2) // 2)
-    def _(p):
-        forward_rows([1 + 2 * p, 2 + 2 * p])
-
     pl.semaphore_wait(barrier, n - 1 + n // 2 + 2 * (zcount // 2 - 1) + 2)
 
-    def exchange(src, dst, idx, k):
+    def exchange(src, dst, idx, k, lo, size):
         peer = lax.rem(me + k, n)
         return pltpu.make_async_remote_copy(
-            src_ref=src.at[peer],
-            dst_ref=dst.at[me],
+            src_ref=src.at[peer, pl.ds(lo, size)],
+            dst_ref=dst.at[me, pl.ds(lo, size)],
             send_sem=send_sems.at[idx],
             recv_sem=recv_sems.at[idx],
             device_id=tm_dev(peer),
             device_id_type=MESH,
         )
 
-    def start_exchange(src, dst, idx):
+    def start_exchange(src, dst, idx, lo=0, size=64):
         @pl.loop(0, n // 2)
         def _(k):
-            exchange(src, dst, idx, 2 * k + 1).start()
+            exchange(src, dst, idx, 2 * k + 1, lo, size).start()
 
         @pl.loop(1, n // 2)
         def _(k):
-            exchange(src, dst, idx, 2 * k).start()
-
-        dst[me] = src[me]
-
-    def all_of(buf, count, idx):
-        view = buf.at[pl.ds(0, count)]
+            exchange(src, dst, idx, 2 * k, lo, size).start()
+
+        dst[me, lo : lo + size] = src[me, lo : lo + size]
+
+    def all_of(buf, idx, lo=0, size=64):
+        view = buf.at[pl.ds(0, n - 1), pl.ds(lo, size)]
         return pltpu.make_async_remote_copy(
             src_ref=view,
             dst_ref=view,
@@ -277,21 +304,28 @@
 
     start_halo(xp, 0)
     start_exchange(cot_t, rcot, 4)
+
+    @pl.loop(0, (n - 2) // 2, unroll=3)
+    def _(p):
+        forward_rows([1 + 2 * p, 2 + 2 * p])
+
     finish_halo(xp, 0)
     load_taps(0)
     load_taps(n - 1)
     forward_rows([0, n - 1])
-    start_exchange(act_t, ract, 5)
-
+    half = ch // 2
+    start_exchange(act_t, ract, 5, 0, half)
+
+    columns = temporal_ref[...].astype(F32).T
     for lag in range(n):
-        kb[lag] = jnp.broadcast_to(temporal_ref[:, lag : lag + 1].astype(F32), (ch, LANES))
+        kb[lag] = jnp.broadcast_to(columns[:, lag : lag + 1], (ch, LANES))
 
     def chan(c):
         return pl.ds(pl.multiple_of(c * 8, 8), 8)
 
-    all_of(rcot, n - 1, 4).wait_recv()
-
-    @pl.loop(0, n)
+    all_of(rcot, 4).wait_recv()
+
+    @pl.loop(0, n, unroll=4)
     def _(t):
         yf[t] = rcot[t].astype(F32)
 
@@ -302,45 +336,50 @@
 
         causal_sums(n, lambda t: yf[n - 1 - t, chan(c), :], lambda lag: kb[lag, chan(c), :], put)
 
-    @pl.loop(0, n)
+    @pl.loop(0, n, unroll=4)
     def _(t):
         back_t[t] = outf[t].astype(BF16)
 
     start_exchange(back_t, rback, 6)
-
-    all_of(ract, n - 1, 5).wait_recv()
-
-    @pl.loop(0, n)
-    def _(t):
-        xf[t] = ract[t].astype(F32)
-
-    @pl.loop(0, ch // 8)
-    def _(c):
-        def put(t, v):
-            outf[t, chan(c), :] = v
-
-        causal_sums(n, lambda t: xf[t, chan(c), :], lambda lag: kb[lag, chan(c), :], put)
-
-    @pl.loop(0, n)
-    def _(t):
-        along_t[t] = outf[t].astype(BF16)
-
-    start_exchange(along_t, ralong, 7)
-
-    lane8 = lax.broadcasted_iota(jnp.int32, (8, 2 * LANES), 1)
-
-    @pl.loop(0, ch // 8)
-    def _(c):
-        total = [jnp.zeros((8, 2 * LANES), F32)]
-
-        def put(lag, v):
-            row = jnp.sum(v, axis=1, keepdims=True)
-            total[0] = jnp.where(lane8 == lag, row, total[0])
-
-        lag_sums(n, lambda t: yf[t, chan(c), :], lambda r: xf[r, chan(c), :], put)
-        kgbuf[chan(c), :] = total[0]
-
-    all_of(rback, n - 1, 6).wait_recv()
+    start_exchange(act_t, ract, 11, half, half)
+
+    lane8 = lax.broadcasted_iota(jnp.int32, (8, LANES), 1)
+
+    def along_half(h, in_idx, out_idx):
+        lo = h * half
+        all_of(ract, in_idx, lo, half).wait_recv()
+
+        @pl.loop(0, n, unroll=4)
+        def _(t):
+            xf[t, lo : lo + half] = ract[t, lo : lo + half].astype(F32)
+
+        @pl.loop(h * (half // 8), (h + 1) * (half // 8))
+        def _(c):
+            def put(t, v):
+                outf[t, chan(c), :] = v
+
+            causal_sums(n, lambda t: xf[t, chan(c), :], lambda lag: kb[lag, chan(c), :], put)
+
+        @pl.loop(0, n, unroll=4)
+        def _(t):
+            along_t[t, lo : lo + half] = outf[t, lo : lo + half].astype(BF16)
+
+        start_exchange(along_t, ralong, out_idx, lo, half)
+
+        @pl.loop(h * (half // 8), (h + 1) * (half // 8))
+        def _(c):
+            total = [jnp.zeros((8, LANES), F32)]
+
+            def put(lag, v):
+                row = jnp.sum(v, axis=1, keepdims=True)
+                total[0] = jnp.where(lane8 == lag, row, total[0])
+
+            lag_sums(n, lambda t: yf[t, chan(c), :], lambda r: xf[r, chan(c), :], put)
+            kgbuf[chan(c), :] = total[0]
+
+    along_half(0, 5, 7)
+
+    all_of(rback, 6).wait_recv()
 
     def gate_row(s):
         v = rback[s].astype(F32) * gbuf[s]
@@ -353,24 +392,31 @@
     gate_row(n - 1)
     start_halo(dp, 2)
 
-    @pl.loop(1, n - 1)
+    @pl.loop(1, n - 1, unroll=5 if (n - 2) % 5 == 0 else 2)
     def _(s):
         gate_row(s)
 
     grads = lax.dot_general(
         db[...], x3[...], (((1,), (1,)), ((), ())), preferred_element_type=F32
     )
-    per = 192 // n
-    kper = ch // n
-    grads = jnp.concatenate([grads, jnp.zeros((192, 64), F32)], axis=1)
-    for k in range(n):
-        red[k, 0:per, :] = grads[k * per : (k + 1) * per]
-        red[k, per : per + kper, :] = kgbuf[k * kper : (k + 1) * kper, :]
+    per = 32 // n
+    used = 9 * per
+    pad = (used + 7) // 8 * 8
+    for a in range(3):
+        for b in range(3):
+            tap = grads[b * ch : (b + 1) * ch, a * ch : (a + 1) * ch]
+            tap = jnp.concatenate([tap[: ch // 2], tap[ch // 2 :]], axis=1)
+            for j in range(per):
+                at = (a * 3 + b) * per + j
+                red[pl.ds(at, n, stride=pad), :] = tap[j * n : (j + 1) * n]
+
+    def chunk(buf, k):
+        return buf.at[pl.ds(pl.multiple_of(k * pad, pad), used)]
 
     def plane_copy(src, dst, idx, peer):
         return pltpu.make_async_remote_copy(
             src_ref=src,
-            dst_ref=dst.at[pi],
+            dst_ref=dst,
             send_sem=send_sems.at[idx],
             recv_sem=recv_sems.at[idx],
             device_id=plane_dev(peer),
@@ -380,92 +426,156 @@
     @pl.loop(1, n)
     def _(k):
         peer = lax.rem(pi + k, n)
-        plane_copy(red.at[peer], rred, 8, peer).start()
-
-    rred[pi] = red[pi]
+        plane_copy(chunk(red, peer), rred.at[pi, pl.ds(0, used)], 8, peer).start()
+
+    rred[pi, 0:used, :] = red[pl.ds(pl.multiple_of(pi * pad, pad), used), :]
 
     def backward_rows(rows):
         taps = jnp.concatenate(
             [jnp.concatenate([dp[s + j] for j in range(3)], axis=0) for s in rows], axis=1
         )
-        out = jnp.dot(wb_ref[...], taps, preferred_element_type=F32)
+        out = jnp.dot(wb[...], taps, preferred_element_type=F32)
         for k, s in enumerate(rows):
             o = out[:, k * LANES : (k + 1) * LANES]
             igf[pl.ds(pl.multiple_of(s * ch, ch), ch), :] = (
                 o[ch : 2 * ch] + left(o[:ch]) + right(o[2 * ch :])
             )
 
-    @pl.loop(0, (n - 2) // 2)
+    @pl.loop(0, (n - 2) // 2, unroll=3)
     def _(p):
         backward_rows([1 + 2 * p, 2 + 2 * p])
 
-    all_of(rred, n - 1, 8).wait_recv()
-    part[...] = jnp.sum(rred[...], axis=0)
-
-    def z_copy(k):
-        peer = lax.rem(zi + k, zcount)
+    along_half(1, 11, 12)
+    lags = kgbuf[...].T[:n]
+    kz[zi] = jnp.concatenate([lags[: n // 2], lags[n // 2 :]], axis=1)
+
+    def lag_z(k):
         return pltpu.make_async_remote_copy(
-            src_ref=part,
-            dst_ref=zpart.at[zi],
+            src_ref=kz.at[zi],
+            dst_ref=kz.at[zi],
+            send_sem=send_sems.at[13],
+            recv_sem=recv_sems.at[13],
+            device_id=z_dev(lax.rem(zi + k, zcount)),
+            device_id_type=MESH,
+        )
+
+    @pl.loop(1, zcount)
+    def _(k):
+        lag_z(k).start()
+
+    def many(buf, count, idx):
+        view = buf.at[pl.ds(0, count)]
+        return plane_copy(view, view, idx, lax.rem(pi + 1, n))
+
+    def all_chunks(buf, count, idx):
+        view = buf.at[pl.ds(0, count), pl.ds(0, used)]
+        return plane_copy(view, view, idx, lax.rem(pi + 1, n))
+
+    all_chunks(rred, n - 1, 8).wait_recv()
+    part[0:used, :] = jnp.sum(rred[:, 0:used, :], axis=0)
+
+    @pl.loop(1, zcount)
+    def _(k):
+        pltpu.make_async_remote_copy(
+            src_ref=part.at[pl.ds(0, used)],
+            dst_ref=zpart.at[zi, pl.ds(0, used)],
             send_sem=send_sems.at[9],
             recv_sem=recv_sems.at[9],
-            device_id=z_dev(peer),
+            device_id=z_dev(lax.rem(zi + k, zcount)),
             device_id_type=MESH,
-        )
-
-    @pl.loop(1, zcount)
-    def _(k):
-        z_copy(k).start()
-
-    zpart[zi] = part[...]
+        ).start()
+
+    zpart[zi, 0:used, :] = part[0:used, :]
+
+    many(kz, zcount - 1, 13).wait_recv()
+    kp[pi] = jnp.sum(kz[...], axis=0) * gscale
+
+    @pl.loop(1, n)
+    def _(k):
+        plane_copy(kp.at[pi], kp.at[pi], 14, lax.rem(pi + k, n)).start()
 
     finish_halo(dp, 2)
     backward_rows([0, n - 1])
 
-    all_of(zpart, zcount - 1, 9).wait_recv()
-    full[...] = jnp.sum(zpart[...], axis=0) * gscale
+    all_chunks(zpart, zcount - 1, 9).wait_recv()
+    full[0:used, :] = jnp.sum(zpart[:, 0:used, :], axis=0) * gscale
 
     @pl.loop(1, n)
     def _(k):
         peer = lax.rem(pi + k, n)
-        plane_copy(full, gathered, 10, peer).start()
-
-    gathered[pi] = full[...]
-
-    @pl.loop(0, ch)
+        plane_copy(full.at[pl.ds(0, used)], chunk(gathered, pi), 10, peer).start()
+
+    gathered[pl.ds(pl.multiple_of(pi * pad, pad), used), :] = full[0:used, :]
+
+    @pl.loop(0, ch, unroll=8)
     def _(c):
         input_grad_ref[0, c] = (
             cot_ref[0, c].astype(F32) + igf[pl.ds(c, n, stride=ch), :]
         ).astype(BF16)
 
-    all_of(ralong, n - 1, 7).wait_recv()
-
-    @pl.loop(0, n)
+    all_of(ralong, 7, 0, half).wait_recv()
+    all_of(ralong, 12, half, half).wait_recv()
+
+    @pl.loop(0, n, unroll=4)
     def _(r):
         tmp[pl.ds(pl.multiple_of(r * ch, ch), ch), :] = ralong[r].astype(F32)
 
-    @pl.loop(0, ch)
+    @pl.loop(0, ch, unroll=8)
     def _(c):
         block_ref[0, c] = (
             frames_ref[0, c].astype(F32) + tmp[pl.ds(c, n, stride=ch), :]
         ).astype(BF16)
 
-    all_of(gathered, n - 1, 10).wait_recv()
-    whole = jnp.concatenate([gathered[k, 0:per, :] for k in range(n)], axis=0)
+    many(kp, n - 1, 14).wait_recv()
+    lags = jnp.sum(kp[...], axis=0)
+    kernel_grad_ref[...] = jnp.concatenate([lags[:, :ch], lags[:, ch:]], axis=0)
+
+    all_chunks(rred, n - 1, 10).wait_recv()
     for a in range(3):
         for b in range(3):
-            weight_grad_ref[a, b] = whole[b * ch : (b + 1) * ch, a * ch : (a + 1) * ch]
-    kernel_grad_ref[...] = jnp.concatenate(
-        [gathered[k, per : per + kper, 0:n] for k in range(n)], axis=0
-    )
-
-    all_of(rcot, n - 1, 4).wait_send()
-    all_of(ract, n - 1, 5).wait_send()
-    all_of(rback, n - 1, 6).wait_send()
-    all_of(ralong, n - 1, 7).wait_send()
-    all_of(rred, n - 1, 8).wait_send()
-    all_of(zpart, zcount - 1, 9).wait_send()
-    all_of(gathered, n - 1, 10).wait_send()
+            rows = []
+            for j in range(per):
+                at = (a * 3 + b) * per + j
+                rows.append(gathered[pl.ds(at, n, stride=pad), :])
+            tap = jnp.concatenate(rows, axis=0)
+            weight_grad_ref[a, b] = jnp.concatenate([tap[:, :ch], tap[:, ch:]], axis=0)
+
+    all_of(rcot, 4).wait_send()
+    all_of(ract, 5, 0, half).wait_send()
+    all_of(ract, 11, half, half).wait_send()
+    all_of(rback, 6).wait_send()
+    all_of(ralong, 7, 0, half).wait_send()
+    all_of(ralong, 12, half, half).wait_send()
+    many(kz, zcount - 1, 13).wait_send()
+    many(kp, n - 1, 14).wait_send()
+    all_chunks(rred, n - 1, 8).wait_send()
+    all_chunks(zpart, zcount - 1, 9).wait_send()
+    all_chunks(rred, n - 1, 10).wait_send()
+
+
+def store_kernel(*refs):
+    count = len(refs) // 2
+    sems = refs[-1]
+    copies = [
+        pltpu.make_async_copy(refs[k], refs[count + k], sems.at[k]) for k in range(count)
+    ]
+    for copy in copies:
+        copy.start()
+    for copy in copies:
+        copy.wait()
+
+
+def store(*arrays):
+    count = len(arrays)
+    return pl.pallas_call(
+        store_kernel,
+        name="store",
+        out_shape=tuple(jax.ShapeDtypeStruct(x.shape, x.dtype) for x in arrays),
+        in_specs=[pl.BlockSpec(memory_space=pl.ANY)] * count,
+        out_specs=(pl.BlockSpec(memory_space=pl.ANY),) * count,
+        scratch_shapes=[pltpu.SemaphoreType.DMA((count,))],
+        compiler_params=pltpu.CompilerParams(vmem_limit_bytes=2**20),
+    )(*arrays)
 
 
 def local(frames, cotangent, spatial_weight, temporal_kernel):
@@ -474,28 +584,32 @@
     _, ch, rows, width = frames.shape
     assert rows == n and ch == 64 and width == LANES and frames.shape[0] == 1
     gscale = float(n * rows * nspan * width) ** (-0.5)
-    wf = spatial_weight.transpose(1, 2, 0, 3).reshape(3 * ch, 3 * ch)
-    wb = spatial_weight[::-1].transpose(1, 3, 0, 2).reshape(3 * ch, 3 * ch)
     block = (n, ch, LANES)
-    red = (n, 256 // n, 256)
+    pad = (9 * (32 // n) + 7) // 8 * 8
 
     def vmem(shape, dtype):
         return pltpu.VMEM(shape, dtype)
 
     spec = pl.BlockSpec(memory_space=pltpu.VMEM)
-    return pl.pallas_call(
+    results = pl.pallas_call(
         functools.partial(kernel, n, nspan, gscale),
         name="space_time_block",
         out_shape=(
             jax.ShapeDtypeStruct(frames.shape, BF16),
             jax.ShapeDtypeStruct(frames.shape, BF16),
             jax.ShapeDtypeStruct((3, 3, ch, ch), F32),
-            jax.ShapeDtypeStruct((ch, n), F32),
+            jax.ShapeDtypeStruct((n, ch), F32),
         ),
-        in_specs=[spec] * 5,
+        in_specs=[pl.BlockSpec(memory_space=pltpu.HBM)] * 4,
         out_specs=(spec,) * 4,
         scratch_shapes=[
+            vmem(frames.shape, BF16),
+            vmem(frames.shape, BF16),
+            vmem(spatial_weight.shape, BF16),
+            vmem((n, ch), BF16),
             vmem((n * ch, LANES), F32),
+            vmem((3 * ch, 3 * ch), BF16),
+            vmem((3 * ch, 3 * ch), BF16),
             vmem((n + 2, ch, LANES), BF16),
             vmem((3 * ch, n * LANES), BF16),
             vmem(block, BF16),
@@ -514,20 +628,25 @@
             vmem((n + 2, ch, LANES), BF16),
             vmem((3 * ch, n * LANES), BF16),
             vmem((n * ch, LANES), F32),
-            vmem((ch, 256), F32),
-            vmem(red, F32),
-            vmem(red, F32),
-            vmem(red[1:], F32),
-            vmem((nspan,) + red[1:], F32),
-            vmem(red[1:], F32),
-            vmem(red, F32),
-            pltpu.SemaphoreType.DMA((11,)),
-            pltpu.SemaphoreType.DMA((11,)),
+            vmem((ch, LANES), F32),
+            vmem((nspan, n // 2, LANES), F32),
+            vmem((n, n // 2, LANES), F32),
+            vmem((n * pad, LANES), F32),
+            vmem((n, pad, LANES), F32),
+            vmem((pad, LANES), F32),
+            vmem((nspan, pad, LANES), F32),
+            vmem((pad, LANES), F32),
+            vmem((n * pad, LANES), F32),
+            pltpu.SemaphoreType.DMA((15,)),
+            pltpu.SemaphoreType.DMA((15,)),
+            pltpu.SemaphoreType.DMA((4,)),
         ],
         compiler_params=pltpu.CompilerParams(
-            collective_id=0, has_side_effects=True, vmem_limit_bytes=48 * 2**20
+            collective_id=0, has_side_effects=True, vmem_limit_bytes=52 * 2**20
         ),
-    )(frames, cotangent, wf, wb, temporal_kernel)
+    )(frames, cotangent, spatial_weight, temporal_kernel.T)
+    block_output, input_grad, weight_grad, kernel_grad = store(*results)
+    return block_output, input_grad, weight_grad, kernel_grad.T
 
 
 def solution(mesh):

time: 84.9 us -> 77.9 us (0.918)
  local copies, waits for them, and re-layouts: 5.99 us -> 1.6 us
  Pallas kernels: 78.1 us -> 75.5 us
    pallas_call x1, Pallas kernels: 78.1 us -> 74.4 us  [local(): pl.pallas_call(functools.partial(kernel, n, nspan, gscale), name='space_t...]
    unnamed x10 -> x4, local copies, waits for them, and re-layouts: 3.7 us -> 1.6 us
    transpose x3 -> x0, local copies, waits for them, and re-layouts: 1.29 us -> none  [the longest x2 1.16 us: local(): wb = spatial_weight[::-1].transpose(1, 3, 0, 2).reshape(3 * ch, 3 * ch)]
    pallas_call x0 -> x1, Pallas kernels: none -> 1.1 us  [store(): pl.pallas_call(store_kernel, name='store', out_shape=tuple((jax.ShapeDtyp...]
where the time goes in v2:
time: 77.9 us; the launch traced here: 77.8 us
  Pallas kernels  75.5 us (97%)
  local copies, waits for them, and re-layouts  1.6 us (2%)
    pallas_call x1, Pallas kernels, local(): pl.pallas_call(functools.partial(kernel, n, nspan, gscale), name='space_t...  74.4 us
    unnamed x4, local copies, waits for them, and re-layouts  1.6 us

profile of v2, /device:TPU:1, one launch (start us, length us, event | category | flops | bytes accessed | tf_op | source)
XLA Modules:
  0.0 77.8 jit_solution(14568863196315092915)
XLA Ops:
  0.6 0.0 copy-start
  0.6 0.9 %copy-done = bf16[3,3,64,64]{3,2,1,0:T(8,128)(2,1)S(1)} copy-done((bf16[3,3,64,64]{3,2,1,0:T(8,128)(2,1)S(1)}, bf16[3,3,64,64]{3,2,1,0:T(8,128)(2,1)}, u32[]{:S(2)}) %copy-start) | copy-done | bytes 73752
  1.5 0.0 copy-start.1
  1.5 0.7 copy-done.1
  2.2 74.4 %space_time_block.1 = (bf16[1,64,32,128]{3,2,1,0:T(8,128)(2,1)S(1)}, bf16[1,64,32,128]{3,2,1,0:T(8,128)(2,1)S(1)}, f32[3,3,64,64]{3,2,1,0:T(8,128)S(1)}, f32[32,64]{1,0:T(8,128)S(1)}) custom-call(bf16[1,64,32,128]{3,2,1,0:T(8,128)(2,1)} %frames_hbm.1, bf16[1,64,32,128]{3,2,1,0:T(8,128)(2,1)} %cot_hbm.1, bf16[3,3,64,64]{3,2,1,0:T(8,128)(2,1)S(1)} %copy-done, ...), custom_call_target="tpu_custom_call" | custom-call | tf_op jit(solution)/shard_map/space_time_block/pallas_call | solution.py:594
  76.7 1.1 %store.1 = (bf16[1,64,32,128]{3,2,1,0:T(8,128)(2,1)}, bf16[1,64,32,128]{3,2,1,0:T(8,128)(2,1)}, f32[3,3,64,64]{3,2,1,0:T(8,128)}, f32[32,64]{1,0:T(8,128)}) custom-call(bf16[1,64,32,128]{3,2,1,0:T(8,128)(2,1)S(1)} %get-tuple-element.12.refs_0_, bf16[1,64,32,128]{3,2,1,0:T(8,128)(2,1)S(1)} %get-tuple-element.13.refs_1_, ...), custom_call_target="tpu_custom_call" | custom-call | tf_op jit(solution)/shard_map/store/pallas_call | solution.py:570
Async XLA Ops:
  0.6 0.9 %copy-start = (bf16[3,3,64,64]{3,2,1,0:T(8,128)(2,1)S(1)}, bf16[3,3,64,64]{3,2,1,0:T(8,128)(2,1)}, u32[]{:S(2)}) copy-start(bf16[3,3,64,64]{3,2,1,0:T(8,128)(2,1)} %weight_hbm.1) | copy-start | bytes 221188
  1.5 0.7 copy-start.1

commit v3 on v2

--- a/solution.py
+++ b/solution.py
@@ -175,17 +175,6 @@
     rows_first(cot_ref, cot_t, 0)
     loads[1].wait()
     rows_first(frames_ref, xp, 1)
-    loads[2].wait()
-    loads[3].wait()
-
-    wide = []
-    for b in range(3):
-        wide.append(jnp.concatenate([weight_ref[a, b].astype(F32) for a in range(3)], axis=1))
-    wf[...] = jnp.concatenate(wide, axis=0).astype(BF16)
-    wide = []
-    for j in range(3):
-        wide.append(jnp.concatenate([weight_ref[2 - j, b].astype(F32) for b in range(3)], axis=1))
-    wb[...] = jnp.concatenate(wide, axis=0).T.astype(BF16)
 
     @pl.when(sp == 0)
     def _():
@@ -214,36 +203,38 @@
             act_t[s] = (hidden * sigma).astype(BF16)
             gbuf[s] = sigma * (1.0 + hidden * (1.0 - sigma))
 
-    @pl.loop(1, n - 1, unroll=2)
-    def _(s):
-        load_taps(s)
-
     pl.semaphore_wait(barrier, n - 1 + n // 2 + 2 * (zcount // 2 - 1) + 2)
 
-    def exchange(src, dst, idx, k, lo, size):
+    def exchange(src, dst, idx, k, lo, size, near=None):
         peer = lax.rem(me + k, n)
         return pltpu.make_async_remote_copy(
             src_ref=src.at[peer, pl.ds(lo, size)],
             dst_ref=dst.at[me, pl.ds(lo, size)],
             send_sem=send_sems.at[idx],
-            recv_sem=recv_sems.at[idx],
+            recv_sem=recv_sems.at[idx if near is None else near],
             device_id=tm_dev(peer),
             device_id_type=MESH,
         )
 
-    def start_exchange(src, dst, idx, lo=0, size=64):
-        @pl.loop(0, n // 2)
+    def start_far(src, dst, idx, lo, size, first, last):
+        @pl.loop(first, last)
         def _(k):
             exchange(src, dst, idx, 2 * k + 1, lo, size).start()
 
+    def start_exchange(src, dst, idx, lo=0, size=64, held=0, near=None):
+        start_far(src, dst, idx, lo, size, 0, n // 2 - held)
+
         @pl.loop(1, n // 2)
         def _(k):
-            exchange(src, dst, idx, 2 * k, lo, size).start()
+            exchange(src, dst, idx, 2 * k, lo, size, near).start()
 
         dst[me, lo : lo + size] = src[me, lo : lo + size]
 
-    def all_of(buf, idx, lo=0, size=64):
-        view = buf.at[pl.ds(0, n - 1), pl.ds(lo, size)]
+    def start_held(src, dst, idx, lo, size, held):
+        start_far(src, dst, idx, lo, size, n // 2 - held, n // 2)
+
+    def all_of(buf, idx, lo=0, size=64, count=n - 1):
+        view = buf.at[pl.ds(0, count), pl.ds(lo, size)]
         return pltpu.make_async_remote_copy(
             src_ref=view,
             dst_ref=view,
@@ -303,7 +294,25 @@
             down.wait_send()
 
     start_halo(xp, 0)
-    start_exchange(cot_t, rcot, 4)
+    half = ch // 2
+    start_exchange(cot_t, rcot, 4, 0, half)
+    start_exchange(cot_t, rcot, 15, half, half)
+
+    loads[2].wait()
+    loads[3].wait()
+    wide = []
+    for b in range(3):
+        wide.append(jnp.concatenate([weight_ref[a, b].astype(F32) for a in range(3)], axis=1))
+    wf[...] = jnp.concatenate(wide, axis=0).astype(BF16)
+    wide = []
+    for j in range(3):
+        wide.append(jnp.concatenate([weight_ref[2 - j, b].astype(F32) for b in range(3)], axis=1))
+    wb[...] = jnp.concatenate(wide, axis=0).T.astype(BF16)
+
+    @pl.loop(1, n - 1, unroll=2)
+    def _(s):
+        load_taps(s)
+
 
     @pl.loop(0, (n - 2) // 2, unroll=3)
     def _(p):
@@ -313,8 +322,6 @@
     load_taps(0)
     load_taps(n - 1)
     forward_rows([0, n - 1])
-    half = ch // 2
-    start_exchange(act_t, ract, 5, 0, half)
 
     columns = temporal_ref[...].astype(F32).T
     for lag in range(n):
@@ -323,35 +330,46 @@
     def chan(c):
         return pl.ds(pl.multiple_of(c * 8, 8), 8)
 
-    all_of(rcot, 4).wait_recv()
-
-    @pl.loop(0, n, unroll=4)
-    def _(t):
-        yf[t] = rcot[t].astype(F32)
-
-    @pl.loop(0, ch // 8)
-    def _(c):
-        def put(t, v):
-            outf[n - 1 - t, chan(c), :] = v
-
-        causal_sums(n, lambda t: yf[n - 1 - t, chan(c), :], lambda lag: kb[lag, chan(c), :], put)
-
-    @pl.loop(0, n, unroll=4)
-    def _(t):
-        back_t[t] = outf[t].astype(BF16)
-
-    start_exchange(back_t, rback, 6)
-    start_exchange(act_t, ract, 11, half, half)
+    def back_half(h, in_idx, out_idx):
+        lo = h * half
+        all_of(rcot, in_idx, lo, half).wait_recv()
+
+        @pl.loop(0, n, unroll=4)
+        def _(t):
+            yf[t, lo : lo + half] = rcot[t, lo : lo + half].astype(F32)
+
+        @pl.loop(h * (half // 8), (h + 1) * (half // 8))
+        def _(c):
+            def put(t, v):
+                outf[n - 1 - t, chan(c), :] = v
+
+            causal_sums(
+                n, lambda t: yf[n - 1 - t, chan(c), :], lambda lag: kb[lag, chan(c), :], put
+            )
+
+        @pl.loop(0, n, unroll=4)
+        def _(t):
+            back_t[t, lo : lo + half] = outf[t, lo : lo + half].astype(BF16)
+
+        start_exchange(back_t, rback, out_idx, lo, half, near=17 + h)
+
+    back_half(0, 4, 6)
+    back_half(1, 15, 16)
+    start_exchange(act_t, ract, 5, 0, half)
+    start_exchange(act_t, ract, 11, half, half, held=n * 0 // 32)
 
     lane8 = lax.broadcasted_iota(jnp.int32, (8, LANES), 1)
 
-    def along_half(h, in_idx, out_idx):
+    def take_act(h, in_idx):
         lo = h * half
         all_of(ract, in_idx, lo, half).wait_recv()
 
         @pl.loop(0, n, unroll=4)
         def _(t):
             xf[t, lo : lo + half] = ract[t, lo : lo + half].astype(F32)
+
+    def along_half(h, out_idx, held=0):
+        lo = h * half
 
         @pl.loop(h * (half // 8), (h + 1) * (half // 8))
         def _(c):
@@ -364,8 +382,9 @@
         def _(t):
             along_t[t, lo : lo + half] = outf[t, lo : lo + half].astype(BF16)
 
-        start_exchange(along_t, ralong, out_idx, lo, half)
-
+        start_exchange(along_t, ralong, out_idx, lo, half, held=held)
+
+    def lag_half(h):
         @pl.loop(h * (half // 8), (h + 1) * (half // 8))
         def _(c):
             total = [jnp.zeros((8, LANES), F32)]
@@ -376,10 +395,6 @@
 
             lag_sums(n, lambda t: yf[t, chan(c), :], lambda r: xf[r, chan(c), :], put)
             kgbuf[chan(c), :] = total[0]
-
-    along_half(0, 5, 7)
-
-    all_of(rback, 6).wait_recv()
 
     def gate_row(s):
         v = rback[s].astype(F32) * gbuf[s]
@@ -388,13 +403,21 @@
         db[ch : 2 * ch, row_cols(s)] = v.astype(BF16)
         db[2 * ch :, row_cols(s)] = right(v).astype(BF16)
 
-    gate_row(0)
-    gate_row(n - 1)
+    all_of(rback, 17, 0, half, n // 2 - 1).wait_recv()
+    all_of(rback, 18, half, half, n // 2 - 1).wait_recv()
+
+    @pl.loop(0, n // 2, unroll=4)
+    def _(k):
+        gate_row(2 * k + zh)
+
+    all_of(rback, 6, 0, half, n // 2).wait_recv()
+    all_of(rback, 16, half, half, n // 2).wait_recv()
+
+    @pl.loop(0, n // 2, unroll=4)
+    def _(k):
+        gate_row(2 * k + 1 - zh)
+
     start_halo(dp, 2)
-
-    @pl.loop(1, n - 1, unroll=5 if (n - 2) % 5 == 0 else 2)
-    def _(s):
-        gate_row(s)
 
     grads = lax.dot_general(
         db[...], x3[...], (((1,), (1,)), ((), ())), preferred_element_type=F32
@@ -428,6 +451,7 @@
         peer = lax.rem(pi + k, n)
         plane_copy(chunk(red, peer), rred.at[pi, pl.ds(0, used)], 8, peer).start()
 
+    start_held(act_t, ract, 11, half, half, n * 0 // 32)
     rred[pi, 0:used, :] = red[pl.ds(pl.multiple_of(pi * pad, pad), used), :]
 
     def backward_rows(rows):
@@ -441,27 +465,14 @@
                 o[ch : 2 * ch] + left(o[:ch]) + right(o[2 * ch :])
             )
 
+    take_act(0, 5)
+    along_half(0, 7)
+
     @pl.loop(0, (n - 2) // 2, unroll=3)
     def _(p):
         backward_rows([1 + 2 * p, 2 + 2 * p])
 
-    along_half(1, 11, 12)
-    lags = kgbuf[...].T[:n]
-    kz[zi] = jnp.concatenate([lags[: n // 2], lags[n // 2 :]], axis=1)
-
-    def lag_z(k):
-        return pltpu.make_async_remote_copy(
-            src_ref=kz.at[zi],
-            dst_ref=kz.at[zi],
-            send_sem=send_sems.at[13],
-            recv_sem=recv_sems.at[13],
-            device_id=z_dev(lax.rem(zi + k, zcount)),
-            device_id_type=MESH,
-        )
-
-    @pl.loop(1, zcount)
-    def _(k):
-        lag_z(k).start()
+    lag_half(0)
 
     def many(buf, count, idx):
         view = buf.at[pl.ds(0, count)]
@@ -474,18 +485,45 @@
     all_chunks(rred, n - 1, 8).wait_recv()
     part[0:used, :] = jnp.sum(rred[:, 0:used, :], axis=0)
 
-    @pl.loop(1, zcount)
-    def _(k):
-        pltpu.make_async_remote_copy(
-            src_ref=part.at[pl.ds(0, used)],
-            dst_ref=zpart.at[zi, pl.ds(0, used)],
-            send_sem=send_sems.at[9],
-            recv_sem=recv_sems.at[9],
+    def z_copy(src, dst, idx, k):
+        return pltpu.make_async_remote_copy(
+            src_ref=src,
+            dst_ref=dst,
+            send_sem=send_sems.at[idx],
+            recv_sem=recv_sems.at[idx],
             device_id=z_dev(lax.rem(zi + k, zcount)),
             device_id_type=MESH,
-        ).start()
+        )
+
+    @pl.loop(1, zcount)
+    def _(k):
+        z_copy(part.at[pl.ds(0, used)], zpart.at[zi, pl.ds(0, used)], 9, k).start()
 
     zpart[zi, 0:used, :] = part[0:used, :]
+
+    take_act(1, 11)
+    lag_half(1)
+    lags = kgbuf[...].T[:n]
+    kz[zi] = jnp.concatenate([lags[: n // 2], lags[n // 2 :]], axis=1)
+
+    @pl.loop(1, zcount)
+    def _(k):
+        z_copy(kz.at[zi], kz.at[zi], 13, k).start()
+
+    along_half(1, 12, held=n * 8 // 32)
+
+    finish_halo(dp, 2)
+    backward_rows([0, n - 1])
+
+    all_chunks(zpart, zcount - 1, 9).wait_recv()
+    full[0:used, :] = jnp.sum(zpart[:, 0:used, :], axis=0) * gscale
+
+    @pl.loop(1, n)
+    def _(k):
+        peer = lax.rem(pi + k, n)
+        plane_copy(full.at[pl.ds(0, used)], chunk(gathered, pi), 10, peer).start()
+
+    gathered[pl.ds(pl.multiple_of(pi * pad, pad), used), :] = full[0:used, :]
 
     many(kz, zcount - 1, 13).wait_recv()
     kp[pi] = jnp.sum(kz[...], axis=0) * gscale
@@ -494,18 +532,7 @@
     def _(k):
         plane_copy(kp.at[pi], kp.at[pi], 14, lax.rem(pi + k, n)).start()
 
-    finish_halo(dp, 2)
-    backward_rows([0, n - 1])
-
-    all_chunks(zpart, zcount - 1, 9).wait_recv()
-    full[0:used, :] = jnp.sum(zpart[:, 0:used, :], axis=0) * gscale
-
-    @pl.loop(1, n)
-    def _(k):
-        peer = lax.rem(pi + k, n)
-        plane_copy(full.at[pl.ds(0, used)], chunk(gathered, pi), 10, peer).start()
-
-    gathered[pl.ds(pl.multiple_of(pi * pad, pad), used), :] = full[0:used, :]
+    start_held(along_t, ralong, 12, half, half, n * 8 // 32)
 
     @pl.loop(0, ch, unroll=8)
     def _(c):
@@ -513,18 +540,23 @@
             cot_ref[0, c].astype(F32) + igf[pl.ds(c, n, stride=ch), :]
         ).astype(BF16)
 
-    all_of(ralong, 7, 0, half).wait_recv()
-    all_of(ralong, 12, half, half).wait_recv()
-
-    @pl.loop(0, n, unroll=4)
-    def _(r):
-        tmp[pl.ds(pl.multiple_of(r * ch, ch), ch), :] = ralong[r].astype(F32)
-
-    @pl.loop(0, ch, unroll=8)
-    def _(c):
-        block_ref[0, c] = (
-            frames_ref[0, c].astype(F32) + tmp[pl.ds(c, n, stride=ch), :]
-        ).astype(BF16)
+    def output_half(h, idx):
+        lo = h * half
+        all_of(ralong, idx, lo, half).wait_recv()
+
+        @pl.loop(0, n, unroll=4)
+        def _(r):
+            tmp[pl.ds(pl.multiple_of(r * ch + lo, half), half), :] = ralong[
+                r, lo : lo + half
+            ].astype(F32)
+
+        @pl.loop(lo, lo + half, unroll=8)
+        def _(c):
+            block_ref[0, c] = (
+                frames_ref[0, c].astype(F32) + tmp[pl.ds(c, n, stride=ch), :]
+            ).astype(BF16)
+
+    output_half(0, 7)
 
     many(kp, n - 1, 14).wait_recv()
     lags = jnp.sum(kp[...], axis=0)
@@ -540,12 +572,11 @@
             tap = jnp.concatenate(rows, axis=0)
             weight_grad_ref[a, b] = jnp.concatenate([tap[:, :ch], tap[:, ch:]], axis=0)
 
-    all_of(rcot, 4).wait_send()
-    all_of(ract, 5, 0, half).wait_send()
-    all_of(ract, 11, half, half).wait_send()
-    all_of(rback, 6).wait_send()
-    all_of(ralong, 7, 0, half).wait_send()
-    all_of(ralong, 12, half, half).wait_send()
+    output_half(1, 12)
+
+    for buf, low, high in ((rcot, 4, 15), (rback, 6, 16), (ract, 5, 11), (ralong, 7, 12)):
+        all_of(buf, low, 0, half).wait_send()
+        all_of(buf, high, half, half).wait_send()
     many(kz, zcount - 1, 13).wait_send()
     many(kp, n - 1, 14).wait_send()
     all_chunks(rred, n - 1, 8).wait_send()
@@ -637,14 +668,19 @@
             vmem((nspan, pad, LANES), F32),
             vmem((pad, LANES), F32),
             vmem((n * pad, LANES), F32),
-            pltpu.SemaphoreType.DMA((15,)),
-            pltpu.SemaphoreType.DMA((15,)),
+            pltpu.SemaphoreType.DMA((19,)),
+            pltpu.SemaphoreType.DMA((19,)),
             pltpu.SemaphoreType.DMA((4,)),
         ],
         compiler_params=pltpu.CompilerParams(
-            collective_id=0, has_side_effects=True, vmem_limit_bytes=52 * 2**20
+            collective_id=0, has_side_effects=True, vmem_limit_bytes=50 * 2**20
         ),
-    )(frames, cotangent, spatial_weight, temporal_kernel.T)
+    )(
+        *[
+            pltpu.with_memory_space_constraint(x, pltpu.HBM)
+            for x in (frames, cotangent, spatial_weight, temporal_kernel.T)
+        ]
+    )
     block_output, input_grad, weight_grad, kernel_grad = store(*results)
     return block_output, input_grad, weight_grad, kernel_grad.T
 

time: 77.9 us -> 72.1 us (0.926)
  Pallas kernels: 75.5 us -> 71.4 us
  local copies, waits for them, and re-layouts: 1.6 us -> 0 us
    pallas_call x1, Pallas kernels: 74.4 us -> 70.3 us  [local(): pl.pallas_call(functools.partial(kernel, n, nspan, gscale), name='space_t...]
    unnamed x4 -> x0, local copies, waits for them, and re-layouts: 1.6 us -> none
where the time goes in v3:
time: 72.1 us; the launch traced here: 72 us
  Pallas kernels  71.4 us (99%)
    pallas_call x1, Pallas kernels, local(): pl.pallas_call(functools.partial(kernel, n, nspan, gscale), name='space_t...  70.3 us

profile of v3, /device:TPU:1, one launch (start us, length us, event | category | flops | bytes accessed | tf_op | source)
XLA Modules:
  0.0 72.0 jit_solution(18233290110727723067)
XLA Ops:
  0.6 70.3 %space_time_block.1 = (bf16[1,64,32,128]{3,2,1,0:T(8,128)(2,1)S(1)}, bf16[1,64,32,128]{3,2,1,0:T(8,128)(2,1)S(1)}, f32[3,3,64,64]{3,2,1,0:T(8,128)S(1)}, f32[32,64]{1,0:T(8,128)S(1)}) custom-call(bf16[1,64,32,128]{3,2,1,0:T(8,128)(2,1)} %frames_hbm.1, bf16[1,64,32,128]{3,2,1,0:T(8,128)(2,1)} %cot_hbm.1, bf16[3,3,64,64]{3,2,1,0:T(8,128)(2,1)} %weight_hbm.1, ...), custom_call_target="tpu_custom_call" | custom-call | tf_op jit(solution)/shard_map/space_time_block/pallas_call | solution.py:625
  70.9 1.1 %store.1 = (bf16[1,64,32,128]{3,2,1,0:T(8,128)(2,1)}, bf16[1,64,32,128]{3,2,1,0:T(8,128)(2,1)}, f32[3,3,64,64]{3,2,1,0:T(8,128)}, f32[32,64]{1,0:T(8,128)}) custom-call(bf16[1,64,32,128]{3,2,1,0:T(8,128)(2,1)S(1)} %get-tuple-element.12.refs_0_, bf16[1,64,32,128]{3,2,1,0:T(8,128)(2,1)S(1)} %get-tuple-element.13.refs_1_, ...), custom_call_target="tpu_custom_call" | custom-call | tf_op jit(solution)/shard_map/store/pallas_call | solution.py:601

commit v4 on v3

--- a/solution.py
+++ b/solution.py
@@ -205,13 +205,13 @@
 
     pl.semaphore_wait(barrier, n - 1 + n // 2 + 2 * (zcount // 2 - 1) + 2)
 
-    def exchange(src, dst, idx, k, lo, size, near=None):
+    def exchange(src, dst, idx, k, lo, size):
         peer = lax.rem(me + k, n)
         return pltpu.make_async_remote_copy(
             src_ref=src.at[peer, pl.ds(lo, size)],
             dst_ref=dst.at[me, pl.ds(lo, size)],
             send_sem=send_sems.at[idx],
-            recv_sem=recv_sems.at[idx if near is None else near],
+            recv_sem=recv_sems.at[idx],
             device_id=tm_dev(peer),
             device_id_type=MESH,
         )
@@ -221,20 +221,20 @@
         def _(k):
             exchange(src, dst, idx, 2 * k + 1, lo, size).start()
 
-    def start_exchange(src, dst, idx, lo=0, size=64, held=0, near=None):
+    def start_exchange(src, dst, idx, lo=0, size=64, held=0):
         start_far(src, dst, idx, lo, size, 0, n // 2 - held)
 
         @pl.loop(1, n // 2)
         def _(k):
-            exchange(src, dst, idx, 2 * k, lo, size, near).start()
+            exchange(src, dst, idx, 2 * k, lo, size).start()
 
         dst[me, lo : lo + size] = src[me, lo : lo + size]
 
     def start_held(src, dst, idx, lo, size, held):
         start_far(src, dst, idx, lo, size, n // 2 - held, n // 2)
 
-    def all_of(buf, idx, lo=0, size=64, count=n - 1):
-        view = buf.at[pl.ds(0, count), pl.ds(lo, size)]
+    def all_of(buf, idx, lo=0, size=64):
+        view = buf.at[pl.ds(0, n - 1), pl.ds(lo, size)]
         return pltpu.make_async_remote_copy(
             src_ref=view,
             dst_ref=view,
@@ -294,9 +294,10 @@
             down.wait_send()
 
     start_halo(xp, 0)
-    half = ch // 2
-    start_exchange(cot_t, rcot, 4, 0, half)
-    start_exchange(cot_t, rcot, 15, half, half)
+    half = ch // 4
+    cot_sems, back_sems, act_sems, along_sems = (4, 15, 17, 18), (6, 16, 19, 20), (5, 11, 21, 22), (7, 12, 23, 24)
+    for h in range(4):
+        start_exchange(cot_t, rcot, cot_sems[h], h * half, half)
 
     loads[2].wait()
     loads[3].wait()
@@ -351,12 +352,12 @@
         def _(t):
             back_t[t, lo : lo + half] = outf[t, lo : lo + half].astype(BF16)
 
-        start_exchange(back_t, rback, out_idx, lo, half, near=17 + h)
-
-    back_half(0, 4, 6)
-    back_half(1, 15, 16)
-    start_exchange(act_t, ract, 5, 0, half)
-    start_exchange(act_t, ract, 11, half, half, held=n * 0 // 32)
+        start_exchange(back_t, rback, out_idx, lo, half)
+
+    for h in range(4):
+        back_half(h, cot_sems[h], back_sems[h])
+    for h in range(4):
+        start_exchange(act_t, ract, act_sems[h], h * half, half)
 
     lane8 = lax.broadcasted_iota(jnp.int32, (8, LANES), 1)
 
@@ -395,6 +396,9 @@
 
             lag_sums(n, lambda t: yf[t, chan(c), :], lambda r: xf[r, chan(c), :], put)
             kgbuf[chan(c), :] = total[0]
+
+    for h in range(4):
+        all_of(rback, back_sems[h], h * half, half).wait_recv()
 
     def gate_row(s):
         v = rback[s].astype(F32) * gbuf[s]
@@ -403,21 +407,13 @@
         db[ch : 2 * ch, row_cols(s)] = v.astype(BF16)
         db[2 * ch :, row_cols(s)] = right(v).astype(BF16)
 
-    all_of(rback, 17, 0, half, n // 2 - 1).wait_recv()
-    all_of(rback, 18, half, half, n // 2 - 1).wait_recv()
-
-    @pl.loop(0, n // 2, unroll=4)
-    def _(k):
-        gate_row(2 * k + zh)
-
-    all_of(rback, 6, 0, half, n // 2).wait_recv()
-    all_of(rback, 16, half, half, n // 2).wait_recv()
-
-    @pl.loop(0, n // 2, unroll=4)
-    def _(k):
-        gate_row(2 * k + 1 - zh)
-
+    gate_row(0)
+    gate_row(n - 1)
     start_halo(dp, 2)
+
+    @pl.loop(1, n - 1, unroll=5 if (n - 2) % 5 == 0 else 2)
+    def _(s):
+        gate_row(s)
 
     grads = lax.dot_general(
         db[...], x3[...], (((1,), (1,)), ((), ())), preferred_element_type=F32
@@ -451,7 +447,6 @@
         peer = lax.rem(pi + k, n)
         plane_copy(chunk(red, peer), rred.at[pi, pl.ds(0, used)], 8, peer).start()
 
-    start_held(act_t, ract, 11, half, half, n * 0 // 32)
     rred[pi, 0:used, :] = red[pl.ds(pl.multiple_of(pi * pad, pad), used), :]
 
     def backward_rows(rows):
@@ -465,14 +460,19 @@
                 o[ch : 2 * ch] + left(o[:ch]) + right(o[2 * ch :])
             )
 
-    take_act(0, 5)
-    along_half(0, 7)
+    for h in range(2):
+        take_act(h, act_sems[h])
+        along_half(h, along_sems[h])
 
     @pl.loop(0, (n - 2) // 2, unroll=3)
     def _(p):
         backward_rows([1 + 2 * p, 2 + 2 * p])
 
     lag_half(0)
+    lag_half(1)
+    take_act(2, act_sems[2])
+    along_half(2, along_sems[2])
+    lag_half(2)
 
     def many(buf, count, idx):
         view = buf.at[pl.ds(0, count)]
@@ -501,8 +501,8 @@
 
     zpart[zi, 0:used, :] = part[0:used, :]
 
-    take_act(1, 11)
-    lag_half(1)
+    take_act(3, act_sems[3])
+    lag_half(3)
     lags = kgbuf[...].T[:n]
     kz[zi] = jnp.concatenate([lags[: n // 2], lags[n // 2 :]], axis=1)
 
@@ -510,7 +510,7 @@
     def _(k):
         z_copy(kz.at[zi], kz.at[zi], 13, k).start()
 
-    along_half(1, 12, held=n * 8 // 32)
+    along_half(3, along_sems[3], held=n * 8 // 32)
 
     finish_halo(dp, 2)
     backward_rows([0, n - 1])
@@ -532,7 +532,7 @@
     def _(k):
         plane_copy(kp.at[pi], kp.at[pi], 14, lax.rem(pi + k, n)).start()
 
-    start_held(along_t, ralong, 12, half, half, n * 8 // 32)
+    start_held(along_t, ralong, along_sems[3], 3 * half, half, n * 8 // 32)
 
     @pl.loop(0, ch, unroll=8)
     def _(c):
@@ -556,7 +556,8 @@
                 frames_ref[0, c].astype(F32) + tmp[pl.ds(c, n, stride=ch), :]
             ).astype(BF16)
 
-    output_half(0, 7)
+    for h in range(3):
+        output_half(h, along_sems[h])
 
     many(kp, n - 1, 14).wait_recv()
     lags = jnp.sum(kp[...], axis=0)
@@ -572,11 +573,11 @@
             tap = jnp.concatenate(rows, axis=0)
             weight_grad_ref[a, b] = jnp.concatenate([tap[:, :ch], tap[:, ch:]], axis=0)
 
-    output_half(1, 12)
-
-    for buf, low, high in ((rcot, 4, 15), (rback, 6, 16), (ract, 5, 11), (ralong, 7, 12)):
-        all_of(buf, low, 0, half).wait_send()
-        all_of(buf, high, half, half).wait_send()
+    output_half(3, along_sems[3])
+
+    for buf, sems in ((rcot, cot_sems), (rback, back_sems), (ract, act_sems), (ralong, along_sems)):
+        for h in range(4):
+            all_of(buf, sems[h], h * half, half).wait_send()
     many(kz, zcount - 1, 13).wait_send()
     many(kp, n - 1, 14).wait_send()
     all_chunks(rred, n - 1, 8).wait_send()
@@ -668,8 +669,8 @@
             vmem((nspan, pad, LANES), F32),
             vmem((pad, LANES), F32),
             vmem((n * pad, LANES), F32),
-            pltpu.SemaphoreType.DMA((19,)),
-            pltpu.SemaphoreType.DMA((19,)),
+            pltpu.SemaphoreType.DMA((25,)),
+            pltpu.SemaphoreType.DMA((25,)),
             pltpu.SemaphoreType.DMA((4,)),
         ],
         compiler_params=pltpu.CompilerParams(

time: 72.1 us -> 71.9 us (level)
  no operation moved by 1% of the time
where the time goes in v4:
time: 71.9 us; the launch traced here: 71.8 us
  Pallas kernels  71.1 us (99%)
    pallas_call x1, Pallas kernels, local(): pl.pallas_call(functools.partial(kernel, n, nspan, gscale), name='space_t...  70 us

profile of v4, /device:TPU:1, one launch (start us, length us, event | category | flops | bytes accessed | tf_op | source)
XLA Modules:
  0.0 71.8 jit_solution(10101591978066696330)
XLA Ops:
  0.6 70.0 %space_time_block.1 = (bf16[1,64,32,128]{3,2,1,0:T(8,128)(2,1)S(1)}, bf16[1,64,32,128]{3,2,1,0:T(8,128)(2,1)S(1)}, f32[3,3,64,64]{3,2,1,0:T(8,128)S(1)}, f32[32,64]{1,0:T(8,128)S(1)}) custom-call(bf16[1,64,32,128]{3,2,1,0:T(8,128)(2,1)} %frames_hbm.1, bf16[1,64,32,128]{3,2,1,0:T(8,128)(2,1)} %cot_hbm.1, bf16[3,3,64,64]{3,2,1,0:T(8,128)(2,1)} %weight_hbm.1, ...), custom_call_target="tpu_custom_call" | custom-call | tf_op jit(solution)/shard_map/space_time_block/pallas_call | solution.py:626
  70.7 1.1 %store.1 = (bf16[1,64,32,128]{3,2,1,0:T(8,128)(2,1)}, bf16[1,64,32,128]{3,2,1,0:T(8,128)(2,1)}, f32[3,3,64,64]{3,2,1,0:T(8,128)}, f32[32,64]{1,0:T(8,128)}) custom-call(bf16[1,64,32,128]{3,2,1,0:T(8,128)(2,1)S(1)} %get-tuple-element.12.refs_0_, bf16[1,64,32,128]{3,2,1,0:T(8,128)(2,1)S(1)} %get-tuple-element.13.refs_1_, ...), custom_call_target="tpu_custom_call" | custom-call | tf_op jit(solution)/shard_map/store/pallas_call | solution.py:602

commit v5 on v4

--- a/solution.py
+++ b/solution.py
@@ -464,15 +464,6 @@
         take_act(h, act_sems[h])
         along_half(h, along_sems[h])
 
-    @pl.loop(0, (n - 2) // 2, unroll=3)
-    def _(p):
-        backward_rows([1 + 2 * p, 2 + 2 * p])
-
-    lag_half(0)
-    lag_half(1)
-    take_act(2, act_sems[2])
-    along_half(2, along_sems[2])
-    lag_half(2)
 
     def many(buf, count, idx):
         view = buf.at[pl.ds(0, count)]
@@ -482,6 +473,8 @@
         view = buf.at[pl.ds(0, count), pl.ds(0, used)]
         return plane_copy(view, view, idx, lax.rem(pi + 1, n))
 
+    lag_half(0)
+    lag_half(1)
     all_chunks(rred, n - 1, 8).wait_recv()
     part[0:used, :] = jnp.sum(rred[:, 0:used, :], axis=0)
 
@@ -501,6 +494,9 @@
 
     zpart[zi, 0:used, :] = part[0:used, :]
 
+    take_act(2, act_sems[2])
+    along_half(2, along_sems[2])
+    lag_half(2)
     take_act(3, act_sems[3])
     lag_half(3)
     lags = kgbuf[...].T[:n]
@@ -512,27 +508,32 @@
 
     along_half(3, along_sems[3], held=n * 8 // 32)
 
+
+    all_chunks(zpart, zcount - 1, 9).wait_recv()
+    full[0:used, :] = jnp.sum(zpart[:, 0:used, :], axis=0) * gscale
+
+    @pl.loop(1, n)
+    def _(k):
+        peer = lax.rem(pi + k, n)
+        plane_copy(full.at[pl.ds(0, used)], chunk(gathered, pi), 10, peer).start()
+
+    gathered[pl.ds(pl.multiple_of(pi * pad, pad), used), :] = full[0:used, :]
+
+    many(kz, zcount - 1, 13).wait_recv()
+    kp[pi] = jnp.sum(kz[...], axis=0) * gscale
+
+    @pl.loop(1, n)
+    def _(k):
+        plane_copy(kp.at[pi], kp.at[pi], 14, lax.rem(pi + k, n)).start()
+
+    start_held(along_t, ralong, along_sems[3], 3 * half, half, n * 8 // 32)
+
+    @pl.loop(0, (n - 2) // 2, unroll=3)
+    def _(p):
+        backward_rows([1 + 2 * p, 2 + 2 * p])
+
     finish_halo(dp, 2)
     backward_rows([0, n - 1])
-
-    all_chunks(zpart, zcount - 1, 9).wait_recv()
-    full[0:used, :] = jnp.sum(zpart[:, 0:used, :], axis=0) * gscale
-
-    @pl.loop(1, n)
-    def _(k):
-        peer = lax.rem(pi + k, n)
-        plane_copy(full.at[pl.ds(0, used)], chunk(gathered, pi), 10, peer).start()
-
-    gathered[pl.ds(pl.multiple_of(pi * pad, pad), used), :] = full[0:used, :]
-
-    many(kz, zcount - 1, 13).wait_recv()
-    kp[pi] = jnp.sum(kz[...], axis=0) * gscale
-
-    @pl.loop(1, n)
-    def _(k):
-        plane_copy(kp.at[pi], kp.at[pi], 14, lax.rem(pi + k, n)).start()
-
-    start_held(along_t, ralong, along_sems[3], 3 * half, half, n * 8 // 32)
 
     @pl.loop(0, ch, unroll=8)
     def _(c):

time: 71.9 us -> 70.4 us (0.979)
  Pallas kernels: 71.1 us -> 69.6 us
    pallas_call x1, Pallas kernels: 70 us -> 68.5 us  [local(): pl.pallas_call(functools.partial(kernel, n, nspan, gscale), name='space_t...]
where the time goes in v5:
time: 70.4 us; the launch traced here: 70.3 us
  Pallas kernels  69.6 us (99%)
    pallas_call x1, Pallas kernels, local(): pl.pallas_call(functools.partial(kernel, n, nspan, gscale), name='space_t...  68.5 us

profile of v5, /device:TPU:1, one launch (start us, length us, event | category | flops | bytes accessed | tf_op | source)
XLA Modules:
  0.0 70.3 jit_solution(1609197019838584737)
XLA Ops:
  0.6 68.5 %space_time_block.1 = (bf16[1,64,32,128]{3,2,1,0:T(8,128)(2,1)S(1)}, bf16[1,64,32,128]{3,2,1,0:T(8,128)(2,1)S(1)}, f32[3,3,64,64]{3,2,1,0:T(8,128)S(1)}, f32[32,64]{1,0:T(8,128)S(1)}) custom-call(bf16[1,64,32,128]{3,2,1,0:T(8,128)(2,1)} %frames_hbm.1, bf16[1,64,32,128]{3,2,1,0:T(8,128)(2,1)} %cot_hbm.1, bf16[3,3,64,64]{3,2,1,0:T(8,128)(2,1)} %weight_hbm.1, ...), custom_call_target="tpu_custom_call" | custom-call | tf_op jit(solution)/shard_map/space_time_block/pallas_call | solution.py:627
  69.2 1.1 %store.1 = (bf16[1,64,32,128]{3,2,1,0:T(8,128)(2,1)}, bf16[1,64,32,128]{3,2,1,0:T(8,128)(2,1)}, f32[3,3,64,64]{3,2,1,0:T(8,128)}, f32[32,64]{1,0:T(8,128)}) custom-call(bf16[1,64,32,128]{3,2,1,0:T(8,128)(2,1)S(1)} %get-tuple-element.12.refs_0_, bf16[1,64,32,128]{3,2,1,0:T(8,128)(2,1)S(1)} %get-tuple-element.13.refs_1_, ...), custom_call_target="tpu_custom_call" | custom-call | tf_op jit(solution)/shard_map/store/pallas_call | solution.py:603
